TPU v7x, 256 devices: a whole 4x4x8 slice. The times are simulated.
256 devices in a mesh: stn: 2 (over core), tm: 32 (over x, z_hi, y), ct: 4 (over z_lo).
Axes of the slice: x: 4, y: 4, z: 8 (z_hi: 2, z_lo: 4; z = z_hi * 4 + z_lo), core: 2. Of those that a mesh axis runs over, the one named last changes fastest.
Arguments:
- voltages: bfloat16 [2, 64, 2097152], P(None, ('stn', 'ct'), 'tm'), may hold values from -128 to 127, as said below
- delays: int32 [64], P(('stn', 'ct')), may hold values from 0 to 4095
Outputs:
- visibilities: float32 [2, 4096, 64, 64], P(None, ('tm', 'ct'), 'stn')
Inputs may be any that keep to these rules, and one draw needn't show every extreme that they name: `voltages`: every entry is a whole number.
All inputs are finite; a program needn't handle non-finite values.
Results may differ from a plain program's by a relative error of at most 0.0037.
Values may be sent and summed in bfloat16 or wider, within the bound.
A program may use at most 128 MiB of HBM per device.

v0:
```python
import math

import jax
import jax.numpy as jnp
from jax import lax
from jax.sharding import PartitionSpec as P

CHANNELS = 4096
RADIX = 64
TAPS = 16


def passed_along(block, axis, distance):
    devices = range(lax.axis_size(axis))
    route = [(i - distance, i) for i in devices if i - distance in devices]
    return lax.ppermute(block, axis, route)


def filter_table():
    length = TAPS * CHANNELS
    index = jnp.arange(length, dtype=jnp.int32).astype(jnp.float32)
    centred = (index - length / 2) / CHANNELS
    window = 0.5 - 0.5 * jnp.cos(2.0 * math.pi * index / length)
    factor = 1.0 / (48.0 * math.sqrt(CHANNELS))
    return (jnp.sinc(centred) * window * factor).reshape(TAPS, CHANNELS)


def dft_block(radix):
    steps = jnp.arange(radix, dtype=jnp.int32)
    grid = steps[:, None] * steps[None, :] % radix
    angle = 2.0 * math.pi * grid.astype(jnp.float32) / radix
    cosine = jnp.cos(angle)
    sine = jnp.sin(angle)
    upper = jnp.concatenate([cosine, sine], axis=1)
    lower = jnp.concatenate([-sine, cosine], axis=1)
    return jnp.concatenate([upper, lower], axis=0).astype(jnp.bfloat16)


def twiddles():
    second = CHANNELS // RADIX
    rows = jnp.arange(second, dtype=jnp.int32)
    cols = jnp.arange(RADIX, dtype=jnp.int32)
    grid = rows[:, None] * cols[None, :] % CHANNELS
    angle = 2.0 * math.pi * grid.astype(jnp.float32) / CHANNELS
    return (jnp.cos(angle), jnp.sin(angle))


def filtered(framed, table):
    count = framed.shape[-2] - TAPS + 1
    total = jnp.zeros(framed.shape[:-2] + (count, CHANNELS), jnp.float32)
    for tap in range(TAPS):
        begin = TAPS - 1 - tap
        total = total + table[tap] * framed[..., begin : begin + count, :].astype(jnp.float32)
    return total.astype(jnp.bfloat16)


def transform(branches):
    second = CHANNELS // RADIX
    number = branches.shape[0]
    stacked = branches.reshape(number, 2 * second, RADIX)
    inner = jnp.einsum(
        "kj,nja->nka", dft_block(second), stacked, preferred_element_type=jnp.float32
    )
    inner = inner.reshape(number, 2, second, RADIX)
    tw_cos, tw_sin = twiddles()
    real_part = inner[:, 0] * tw_cos + inner[:, 1] * tw_sin
    imag_part = inner[:, 1] * tw_cos - inner[:, 0] * tw_sin
    turned = (
        jnp.stack([real_part, imag_part], axis=2)
        .reshape(number, second, 2 * RADIX)
        .astype(jnp.bfloat16)
    )
    result = jnp.einsum("lj,nkj->nlk", dft_block(RADIX), turned, preferred_element_type=jnp.float32)
    return result.reshape(number, 2, CHANNELS).astype(jnp.bfloat16)


def pick_span(row, offset, span):
    return lax.dynamic_slice_in_dim(row, CHANNELS - offset, span, 1)


def on_device(voltages, delays):
    in_count = voltages.shape[1]
    frame_count = voltages.shape[2] // CHANNELS
    prior = passed_along(voltages, "tm", 1)
    extended = jnp.concatenate([prior, voltages], axis=2)
    span = (frame_count + TAPS - 1) * CHANNELS
    shifted = jax.vmap(
        lambda row, offset: pick_span(row, offset, span), in_axes=(1, 0), out_axes=1
    )(extended, delays)
    framed = shifted.reshape(2, in_count, frame_count + TAPS - 1, CHANNELS)
    branches = jnp.moveaxis(filtered(framed, filter_table()), 0, 2)
    spectra = transform(branches.reshape(in_count * frame_count, 2, CHANNELS))
    spectra = spectra.reshape(in_count, frame_count, 2, CHANNELS)
    moved = lax.all_to_all(
        lax.all_to_all(spectra, "tm", split_axis=3, concat_axis=1, tiled=True),
        "ct",
        split_axis=3,
        concat_axis=0,
        tiled=True,
    )
    local = moved.transpose(3, 2, 0, 1)
    total_frames = local.shape[3]
    swapped = jnp.stack([local[:, 1], -local[:, 0]], axis=1)
    left = jnp.stack([local, swapped], axis=0)
    summed = jnp.einsum(
        "ocjaf,cjbf->ocab",
        left,
        lax.all_gather(local, "stn", axis=2, tiled=True),
        preferred_element_type=jnp.float32,
    )
    return summed * (1.0 / total_frames)


def solution(mesh):
    return jax.shard_map(
        on_device,
        mesh=mesh,
        in_specs=(P(None, ("stn", "ct"), "tm"), P(("stn", "ct"))),
        out_specs=P(None, ("tm", "ct"), "stn", None),
        check_vma=False,
    )
```

profile of v0, /device:TPU:1, one launch (start us, length us, event | category | flops | bytes accessed | tf_op | source)
XLA Modules:
  0.0 411.2 jit_solution(17613483547774946661)
XLA Ops:
  6.5 0.0 all-gather.2.cloned.1.call-start
  6.5 3.8 copy.57
  10.3 5.4 %collective-permute-start = (bf16[2,8,65536]{2,0,1:T(2,128)(2,1)S(1)}, bf16[2,8,65536]{2,0,1:T(2,128)(2,1)}, u32[]{:S(2)}, u32[]{:S(2)}) collective-permute-start(bf16[2,8,65536]{2,0,1:T(2,128)(2,1)S(1)} %copy.57), channel_id=1, source_target_pairs={{0,4},{4,8},{8,12},{12,16},{16,20},{20,24},{24,28},{28,32},{32,36}... | collective-permute-start | bytes 6291464 | tf_op jit(solution)/shard_map/ppermute | solution.py:16
  15.7 0.0 copy-done.1
  15.7 0.1 fusion.49
  15.9 0.2 negate_convert_fusion
  16.0 0.1 fusion.46
  16.2 1.2 fusion.34
  17.4 41.2 %collective-permute-done = bf16[2,8,65536]{2,0,1:T(2,128)(2,1)} collective-permute-done((bf16[2,8,65536]{2,0,1:T(2,128)(2,1)S(1)}, bf16[2,8,65536]{2,0,1:T(2,128)(2,1)}, u32[]{:S(2)}, u32[]{:S(2)}) %collective-permute-start) | collective-permute-done | bytes 2097184 | tf_op jit(solution)/shard_map/ppermute | solution.py:16
  58.6 7.1 %maximum_bitcast_fusion = bf16[8,2,131072]{2,1,0:T(2,128)(2,1)} fusion(bf16[2,8,65536]{2,0,1:T(2,128)(2,1)S(1)} %copy.57, bf16[2,8,65536]{2,0,1:T(2,128)(2,1)} %collective-permute-done), kind=kLoop, calls=%fused_computation.2 | loop fusion | flops 8388608 | bytes 8388608 | tf_op jit(solution)/shard_map/vmap()/transpose | solution.py:78
  65.8 34.8 %while.1 = (s32[]{:T(128)}, bf16[8,2,131072]{2,1,0:T(2,128)(2,1)}, s32[8,3]{0,1:T(4,128)S(1)}, bf16[8,2,126976]{2,1,0:T(2,128)(2,1)}, s32[]{:T(128)}) while((s32[]{:T(128)}, bf16[8,2,131072]{2,1,0:T(2,128)(2,1)}, s32[8,3]{0,1:T(4,128)S(1)}, bf16[8,2,126976]{2,1,0:T(2,128)(2,1)}, s32[]{:T(128)}) %tuple.41), condition=%wide.while_cond, body=%wide.while_body.sunk | while | flops 2 | bytes 1016949 | solution.py:78
  65.8 0.1 constant_dynamic-slice_fusion.2
  65.8 0.6 fusion.62
  66.4 3.7 dynamic-slice_dynamic-update-slice_fusion.2
  70.1 0.1 constant_dynamic-slice_fusion.2
  70.2 0.6 fusion.62
  70.7 3.7 dynamic-slice_dynamic-update-slice_fusion.2
  74.4 0.1 constant_dynamic-slice_fusion.2
  74.5 0.6 fusion.62
  75.1 3.7 dynamic-slice_dynamic-update-slice_fusion.2
  78.8 0.1 constant_dynamic-slice_fusion.2
  78.9 0.6 fusion.62
  79.5 3.7 dynamic-slice_dynamic-update-slice_fusion.2
  83.2 0.1 constant_dynamic-slice_fusion.2
  83.2 0.6 fusion.62
  83.8 3.7 dynamic-slice_dynamic-update-slice_fusion.2
  87.5 0.1 constant_dynamic-slice_fusion.2
  87.6 0.6 fusion.62
  88.2 3.7 dynamic-slice_dynamic-update-slice_fusion.2
  91.9 0.1 constant_dynamic-slice_fusion.2
  91.9 0.6 fusion.62
  92.5 3.7 dynamic-slice_dynamic-update-slice_fusion.2
  96.2 0.1 constant_dynamic-slice_fusion.2
  96.3 0.6 fusion.62
  96.8 3.7 dynamic-slice_dynamic-update-slice_fusion.2
  100.6 4.4 %copy.59 = bf16[8,2,126976]{2,0,1:T(8,128)(2,1)S(1)} copy(bf16[8,2,126976]{2,1,0:T(2,128)(2,1)} %get-tuple-element.12) | data formatting | bytes 8126464 | tf_op jit(solution)/shard_map/vmap()/gather | solution.py:78
  105.0 8.8 %fusion.5 = bf16[8,16,2,4096]{3,0,1,2:T(8,128)(2,1)S(1)} fusion(bf16[2,8,31,4096]{3,1,2,0:T(8,128)(2,1)S(1)} %bitcast.81, f32[4096]{0:T(1024)S(1)} %get-tuple-element.32, f32[4096]{0:T(1024)S(1)} %get-tuple-element.33, f32[4096]{0:T(1024)S(1)} %get-tuple-element.34, f32[4096]{0:T(1024)S(1)} %get-tuple-element.35, f32[4096]{0:T(1024)S(1)} %get-tuple-element.36, ...), kind=kLoop, calls=%fused_computation.16 | loop fusion | flops 50331648 | bytes 35913728 | tf_op jit(solution)/shard_map/transpose | solution.py:91
  113.8 2.2 copy.60
  116.0 4.2 %reshape_reshape.3 = bf16[128,128,64]{2,1,0:T(8,128)(2,1)} reshape(bf16[8,16,2,4096]{3,2,1,0:T(2,128)(2,1)S(1)} %copy.60) | data formatting | bytes 4194304 | tf_op jit(solution)/shard_map/reshape;reshape | solution.py:60
  120.1 4.8 %copy.61 = bf16[128,128,64]{1,0,2:T(8,128)(2,1)S(1)} copy(bf16[128,128,64]{2,1,0:T(8,128)(2,1)} %reshape_reshape.3) | data formatting | bytes 4194304 | tf_op jit(solution)/shard_map/reshape;reshape | solution.py:60
  124.9 0.8 fusion.50
  125.7 0.6 fusion.56
  126.3 5.0 %add_convert_fusion.1 = (bf16[128,64,1,64]{0,3,2,1:T(8,128)(2,1)S(1)}, bf16[128,64,1,64]{0,3,2,1:T(8,128)(2,1)S(1)}) fusion(f32[128,1,64,64]{0,2,1,3:T(8,128)S(1)} %get-tuple-element.26, f32[128,1,64,64]{0,2,1,3:T(8,128)S(1)} %get-tuple-element.25, f32[64,64]{1,0:T(8,128)S(1)} %get-tuple-element.49, f32[64,64]{1,0:T(8,128)S(1)} %get-tuple-element.50), kind=kLoop, calls=%fused_computation.15 | loop fusion | flops 4194304 | bytes 6324224 | tf_op jit(solution)/shard_map/convert
  131.3 0.2 pad_maximum_fusion
  131.5 0.8 convert_bitcast_fusion
  132.3 3.9 copy.65
  136.2 6.7 %convert_element_type.154 = bf16[8,16,2,4096]{3,2,1,0:T(2,128)(2,1)S(1)} reshape(bf16[128,128,64]{2,1,0:T(8,128)(2,1)} %copy.65) | data formatting | bytes 4194304 | tf_op jit(solution)/shard_map/convert_element_type | solution.py:74
  142.9 16.7 %copy.66 = bf16[8,16,2,4096]{1,0,2,3:T(8,128)(2,1)} copy(bf16[8,16,2,4096]{3,2,1,0:T(2,128)(2,1)S(1)} %convert_element_type.154) | data formatting | bytes 4194304 | tf_op jit(solution)/shard_map/convert_element_type | solution.py:74
  159.6 19.7 %reshape.171 = bf16[32,2,16384]{2,1,0:T(2,128)(2,1)S(1)} reshape(bf16[4096,2,8,16]{3,2,1,0:T(8,128)(2,1)} %bitcast.82) | data formatting | bytes 4194304
  179.4 59.7 %all_to_all.36 = bf16[32,2,16384]{2,1,0:T(2,128)(2,1)} all-to-all(bf16[32,2,16384]{2,1,0:T(2,128)(2,1)S(1)} %reshape.171), channel_id=1, replica_groups=mesh['stn'=2,'tm'=32,'ct'=4] {'tm'}, dimensions={0} | all-to-all | bytes 4194304 | tf_op jit(solution)/shard_map/all_to_all | solution.py:95
  239.1 16.5 %reshape.172 = bf16[4096,2,8,16]{3,2,1,0:T(8,128)(2,1)} reshape(bf16[32,2,16384]{2,1,0:T(2,128)(2,1)} %all_to_all.36) | data formatting | bytes 4194304
  255.5 15.3 %copy.68 = bf16[8,32,16,2,128]{4,2,1,3,0:T(8,128)(2,1)S(1)} copy(bf16[8,32,16,2,128]{2,0,3,4,1:T(8,128)(2,1)} %bitcast.83) | data formatting | bytes 4194304 | tf_op jit(solution)/shard_map/all_to_all | solution.py:95
  270.8 4.0 copy.69
  274.8 104.3 %all_to_all.37 = bf16[8,512,2,128]{1,2,0,3:T(2,128)(2,1)S(1)} all-to-all(bf16[8,512,2,128]{1,2,0,3:T(2,128)(2,1)} %copy.69), channel_id=1, replica_groups=mesh['stn'=2,'tm'=32,'ct'=4] {'ct'}, dimensions={3} | all-to-all | bytes 4194304 | tf_op jit(solution)/shard_map/all_to_all | solution.py:94
  379.1 1.2 copy.70
  380.2 2.5 copy.93
  382.7 0.0 all-gather.2.cloned.1.call-update
  382.8 0.0 copy-start
  382.8 1.8 fusion.57
  384.6 1.5 maximum_bitcast_fusion.1
  386.2 13.0 %all-gather.2.cloned.1.call-done = bf16[32,2,64,512]{3,2,1,0:T(8,128)(2,1)} async-done(((bf16[32,2,32,512]{3,2,1,0:T(8,128)(2,1)}), bf16[32,2,64,512]{3,2,1,0:T(8,128)(2,1)}) %all-gather.2.cloned.1.call-update) | async-done | bytes 4194320 | tf_op jit(solution)/shard_map/all_gather | solution.py:108
  399.1 0.0 copy-done
  399.1 4.1 fusion.16
  403.3 1.1 copy.73
  (6 shorter events, 0.0 us)
Async XLA Ops:
  6.5 9.2 %copy-start.1 = (s32[8]{0:T(128)S(1)}, s32[8]{0:T(128)}, u32[]{:S(2)}) copy-start(s32[8]{0:T(128)} %param.3) | copy-start | bytes 100
  6.5 392.6 %all-gather.2.cloned.1.call-start = ((), (), s32[]{:S(2)}) async-start(), calls=%async_computation.2 | async-start | bytes 6291456 | tf_op jit(solution)/shard_map/all_gather | solution.py:108
  10.3 48.3 %collective-permute-start = (bf16[2,8,65536]{2,0,1:T(2,128)(2,1)S(1)}, bf16[2,8,65536]{2,0,1:T(2,128)(2,1)}, u32[]{:S(2)}, u32[]{:S(2)}) collective-permute-start(bf16[2,8,65536]{2,0,1:T(2,128)(2,1)S(1)} %copy.57), channel_id=1, source_target_pairs={{0,4},{4,8},{8,12},{12,16},{16,20},{20,24},{24,28},{28,32},{32,36}... | collective-permute-start | bytes 6291464 | tf_op jit(solution)/shard_map/ppermute | solution.py:16
  382.8 16.4 %copy-start = (bf16[4,8,512,2,32]{2,1,0,3,4:T(8,128)(2,1)S(1)}, bf16[4,8,512,2,32]{2,1,0,3,4:T(8,128)(2,1)}, u32[]{:S(2)}) copy-start(bf16[4,8,512,2,32]{2,1,0,3,4:T(8,128)(2,1)} %copy.93) | copy-start | bytes 6291460
Sparse Core Ops, SparseCore 0:
  382.9 16.2 all-gather.1
where the time goes:
time: 413 us; the launch traced here: 411 us
  blocking collectives  164 us (40%)
  local copies, waits for them, and re-layouts  142 us (34%)
  waiting for transfers between devices  54.2 us (13%)
  other arithmetic  26.1 us (6%)
  between operations  13.5 us (3%)
  matrix products  5.65 us (1%)
  starting transfers between devices  5.4 us (1%)
    all_to_all x1, blocking collectives, on_device(): lax.all_to_all(lax.all_to_all(spectra, 'tm', split_axis=3, concat_axis=1,...  104 us
    all_to_all x1, blocking collectives, on_device(): lax.all_to_all(spectra, 'tm', split_axis=3, concat_axis=1, tiled=True)  59.7 us
    ppermute x1, waiting for transfers between devices, passed_along(): return lax.ppermute(block, axis, route)  41.2 us
    unnamed x8, local copies, waits for them, and re-layouts  39.9 us
    gather x24, local copies, waits for them, and re-layouts  34.8 us
    convert_element_type x3, local copies, waits for them, and re-layouts, transform(): return result.reshape(number, 2, CHANNELS).astype(jnp.bfloat16)  27.4 us
    all_to_all x2, local copies, waits for them, and re-layouts, on_device(): lax.all_to_all(spectra, 'tm', split_axis=3, concat_axis=1, tiled=True)  19.3 us
    all_gather x1, waiting for transfers between devices, on_device(): lax.all_gather(local, 'stn', axis=2, tiled=True)  13 us
  transfers between devices with their start and end apart: 2, of which 2 were waited for; matrix products, arithmetic and copies ran while one was open for 1% of the time, Pallas kernels for 0%

commit v1 on v0

v1 whole, which is shorter than its diff:
```python
import math

import jax
import jax.numpy as jnp
import numpy as np
from jax import lax
from jax.experimental import pallas as pl
from jax.experimental.pallas import tpu as pltpu
from jax.sharding import PartitionSpec as P

CHANNELS = 4096
TAPS = 16
SLOW = 32
FAST = 128
BLOCK = 16
GROUP = 4
FRAMES = 512


def filter_table():
    length = TAPS * CHANNELS
    index = np.arange(length, dtype=np.float64)
    centred = (index - length / 2) / CHANNELS
    window = 0.5 - 0.5 * np.cos(2.0 * math.pi * index / length)
    factor = 1.0 / (48.0 * math.sqrt(CHANNELS))
    return (np.sinc(centred) * window * factor).reshape(TAPS, CHANNELS).astype(np.float32)


def rolled_filter(delay):
    table = filter_table()
    doubled = jnp.asarray(np.concatenate([table, table], axis=1))
    turned = lax.dynamic_slice(doubled, (0, delay), (TAPS, CHANNELS))
    carry = jnp.arange(CHANNELS, dtype=jnp.int32) + delay >= CHANNELS
    later = jnp.pad(turned, ((1, 7), (0, 0)))
    same = jnp.pad(turned, ((0, 8), (0, 0)))
    taps = jnp.where(carry[None, :], later, same)
    return taps.reshape(24, SLOW, FAST).transpose(1, 0, 2)


def turn_tables(delay):
    k = jnp.arange(SLOW, dtype=jnp.int32)[:, None]
    q = jnp.arange(FAST, dtype=jnp.int32)[None, :]
    angle = (k * (q + delay) % CHANNELS).astype(jnp.float32) * (2.0 * math.pi / CHANNELS)
    return jnp.stack([jnp.cos(angle), jnp.sin(angle)])


def last_table(delay):
    l = jnp.arange(FAST, dtype=jnp.int32)[:, None]
    q = jnp.arange(FAST, dtype=jnp.int32)[None, :]
    angle = (l * (q + delay) % FAST).astype(jnp.float32) * (2.0 * math.pi / FAST)
    cosine, sine = jnp.cos(angle), jnp.sin(angle)
    upper = jnp.concatenate([cosine, sine], axis=1)
    lower = jnp.concatenate([-sine, cosine], axis=1)
    return jnp.concatenate([upper, lower], axis=0).astype(jnp.bfloat16)


def fft(xs):
    n = len(xs)
    if n == 1:
        return xs
    even, odd = fft(xs[0::2]), fft(xs[1::2])
    low, high = [], []
    for k in range(n // 2):
        re, im = odd[k]
        if k == 0:
            tr, ti = re, im
        elif 4 * k == n:
            tr, ti = im, -re
        elif 8 * k == n:
            s = math.sqrt(0.5)
            tr, ti = (re + im) * s, (im - re) * s
        elif 8 * k == 3 * n:
            s = math.sqrt(0.5)
            tr, ti = (im - re) * s, (im + re) * (-s)
        else:
            c, s = math.cos(2 * math.pi * k / n), math.sin(2 * math.pi * k / n)
            tr, ti = re * c + im * s, im * c - re * s
        er, ei = even[k]
        low.append((er + tr, ei + ti))
        high.append((er - tr, ei - ti))
    return low + high


def spectra_kernel(own_ref, halo_ref, taps_ref, turn_ref, last_ref, out_ref, xs, branch, inner, flat):
    @pl.loop(0, 2)
    def _(i):
        @pl.loop(0, SLOW)
        def _(b):
            lanes = pl.ds(pl.multiple_of(b * FAST, FAST), FAST)
            taps = [
                jnp.broadcast_to(taps_ref[i, b, k : k + 1, :], (8, FAST)) for k in range(TAPS + 1)
            ]
            for r in range(2):
                xs[r, 0:BLOCK, :] = halo_ref[i, r, :, lanes].astype(jnp.float32)
                for g in range(GROUP):
                    first = BLOCK * (g + 1)
                    xs[r, first : first + BLOCK, :] = own_ref[g, i, r, :, lanes].astype(jnp.float32)
            for r in range(2):
                total = [None] * 8
                for s in range(-16, 57):
                    window = xs[r, BLOCK + s : BLOCK + s + 8, :]
                    for o in range(8):
                        k = 8 * o - s
                        if 0 <= k <= TAPS:
                            term = taps[k] * window
                            total[o] = term if total[o] is None else total[o] + term
                        if k == 0:
                            branch[r, b, 8 * o : 8 * o + 8, :] = total[o]

        @pl.loop(0, 8)
        def _(o):
            rows = pl.ds(pl.multiple_of(o * 8, 8), 8)
            points = [(branch[0, b, rows, :], branch[1, b, rows, :]) for b in range(SLOW)]
            for k, (re, im) in enumerate(fft(points)):
                c = jnp.broadcast_to(turn_ref[i, 0, k : k + 1, :], (8, FAST))
                s = jnp.broadcast_to(turn_ref[i, 1, k : k + 1, :], (8, FAST))
                inner[k, rows, 0:FAST] = re * c + im * s
                inner[k, rows, FAST : 2 * FAST] = im * c - re * s

        @pl.loop(0, 8)
        def _(g):
            points = inner[pl.ds(g * 4, 4), :, :].reshape(4 * 64, 2 * FAST).astype(jnp.bfloat16)
            result = lax.dot_general(
                last_ref[i], points, (((1,), (1,)), ((), ())), preferred_element_type=jnp.float32
            )
            for r in range(2):
                for t in range(2):
                    for l in range(16):
                        piece = result[
                            r * FAST + 8 * l : r * FAST + 8 * l + 8, t * FAST : t * FAST + FAST
                        ]
                        flat[r, pl.ds(l * 128 + g * 2 + t, 8, stride=16), :] = piece

        @pl.loop(0, FAST, step=8)
        def _(l0):
            for dl in range(8):
                for r in range(2):
                    rows = pl.ds(pl.multiple_of((l0 + dl) * 16, 16), 16)
                    out_ref[l0 + dl, i, r, :, :] = flat[r, rows, :].astype(jnp.bfloat16)


def spectra_of(own, halo, taps, turn, last):
    return pl.pallas_call(
        spectra_kernel,
        out_shape=jax.ShapeDtypeStruct((FAST, 2, 2, 16, FAST), jnp.bfloat16),
        in_specs=[pl.BlockSpec(memory_space=pltpu.VMEM)] * 5,
        out_specs=pl.BlockSpec(memory_space=pltpu.VMEM),
        scratch_shapes=[
            pltpu.VMEM((2, 80, FAST), jnp.float32),
            pltpu.VMEM((2, SLOW, 64, FAST), jnp.float32),
            pltpu.VMEM((SLOW, 64, 2 * FAST), jnp.float32),
            pltpu.VMEM((2, FAST * 16, FAST), jnp.float32),
        ],
        compiler_params=pltpu.CompilerParams(vmem_limit_bytes=48 << 20),
    )(own, halo, taps, turn, last)


def correlate_kernel(got_ref, out_ref, wide, packed):
    mine = lax.axis_index("stn")
    low = lax.broadcasted_iota(jnp.int32, (16, FAST), 1) < 64

    @pl.loop(0, 4)
    def _(pair):
        @pl.loop(0, 2)
        def _(t):
            @pl.loop(0, 2)
            def _(stn):
                for ct in range(4):
                    for y in range(4):
                        for i in range(2):
                            for r in range(2):
                                row = stn * 32 + (ct * 4 + y) * 2 + i
                                source = (pair * 2 + t) * 16 + y * 4 + ct
                                place = pl.ds(pl.multiple_of(row * 16, 16), 16)
                                wide[t, r, place, :] = got_ref[stn, source, i, r, :, :].astype(
                                    jnp.float32
                                )

        @pl.loop(0, 16)
        def _(j):
            for r in range(2):
                for g in range(4):
                    a = jnp.concatenate(
                        [wide[0, r, pl.ds((g * 16 + h * 8) * 16 + j, 8, stride=16), :] for h in range(2)],
                        axis=0,
                    )
                    b = jnp.concatenate(
                        [wide[1, r, pl.ds((g * 16 + h * 8) * 16 + j, 8, stride=16), :] for h in range(2)],
                        axis=0,
                    )
                    lanes = pl.ds(pl.multiple_of(pair * FAST, FAST), FAST)
                    place = slice(r * 64 + g * 16, r * 64 + g * 16 + 16)
                    packed[2 * j, place, lanes] = jnp.where(low, a, pltpu.roll(b, 64, 1)).astype(
                        jnp.bfloat16
                    )
                    packed[2 * j + 1, place, lanes] = jnp.where(low, pltpu.roll(a, 64, 1), b).astype(
                        jnp.bfloat16
                    )

    @pl.loop(0, SLOW)
    def _(k):
        everyone = packed[k]
        left = jnp.concatenate(
            [packed[k, pl.ds(pl.multiple_of(r * 64 + mine * 32, 32), 32), :] for r in range(2)], axis=0
        )
        grid = lax.dot_general(
            left, everyone, (((1,), (1,)), ((), ())), preferred_element_type=jnp.float32
        )
        out_ref[0, k, :, :] = (grid[0:32, 0:64] + grid[32:64, 64:128]) * (1.0 / FRAMES)
        out_ref[1, k, :, :] = (grid[32:64, 0:64] - grid[0:32, 64:128]) * (1.0 / FRAMES)


def correlated(got):
    return pl.pallas_call(
        correlate_kernel,
        out_shape=jax.ShapeDtypeStruct((2, SLOW, 32, 64), jnp.float32),
        in_specs=[pl.BlockSpec(memory_space=pltpu.VMEM)],
        out_specs=pl.BlockSpec(memory_space=pltpu.VMEM),
        scratch_shapes=[
            pltpu.VMEM((2, 2, 64 * 16, FAST), jnp.float32),
            pltpu.VMEM((SLOW, FAST, 4 * FAST), jnp.bfloat16),
        ],
        compiler_params=pltpu.CompilerParams(vmem_limit_bytes=48 << 20),
    )(got)


def on_device(voltages, delays):
    where = lax.axis_index("tm") % GROUP
    mine = lax.dynamic_slice(delays, (2 * where,), (2,))
    taps = jnp.stack([rolled_filter(mine[i]) for i in range(2)])
    turn = jnp.stack([turn_tables(mine[i]) for i in range(2)])
    last = jnp.stack([last_table(mine[i]) for i in range(2)])
    pieces = voltages.reshape(2, GROUP, 2, BLOCK, CHANNELS).transpose(1, 2, 0, 3, 4)
    groups = [[GROUP * g + j for j in range(GROUP)] for g in range(8)]
    own = lax.all_to_all(pieces, "tm", 0, 0, axis_index_groups=groups, tiled=True)
    halo = lax.ppermute(own[GROUP - 1], "tm", [(t, t + GROUP) for t in range(28)])
    chunks = spectra_of(own, halo, taps, turn, last)
    moved = lax.all_to_all(chunks, ("tm", "ct"), 0, 0, tiled=True)
    return correlated(lax.all_gather(moved, "stn", axis=0))


def solution(mesh):
    return jax.shard_map(
        on_device,
        mesh=mesh,
        in_specs=(P(None, ("stn", "ct"), "tm"), P(("stn", "ct"))),
        out_specs=P(None, ("tm", "ct"), "stn", None),
        check_vma=False,
    )
```

time: 413 us -> 192 us (0.46)
  local copies, waits for them, and re-layouts: 142 us -> 7.53 us
  blocking collectives: 164 us -> 73.7 us
  Pallas kernels: 0 us -> 31 us
  other arithmetic: 26.1 us -> 3.65 us
  waiting for transfers between devices: 54.2 us -> 42.9 us
  starting transfers between devices: 5.4 us -> 14.9 us
  matrix products: 5.65 us -> 0 us
    all_to_all x2 -> x1, blocking collectives: 164 us -> 73.7 us  [on_device(): moved = lax.all_to_all(chunks, ('tm', 'ct'), 0, 0, tiled=True)]
    gather x25 -> x0, local copies, waits for them, and re-layouts: 39.2 us -> none
    unnamed x8 -> x7, local copies, waits for them, and re-layouts: 39.9 us -> 4.94 us
    pallas_call x0 -> x2, Pallas kernels: none -> 31 us  [the longest x1 18.2 us: correlated(): pl.pallas_call(correlate_kernel, out_shape=jax.ShapeDtypeStruct((2, SLOW,...]
    ppermute x1, waiting for transfers between devices: 41.2 us -> 11.4 us  [on_device(): lax.ppermute(own[GROUP - 1], 'tm', [(t, t + GROUP) for t in range(28)])]
    convert_element_type x3 -> x0, local copies, waits for them, and re-layouts: 27.4 us -> none  [transform(): return result.reshape(number, 2, CHANNELS).astype(jnp.bfloat16)]
    all_to_all x4 -> x0, local copies, waits for them, and re-layouts: 22.9 us -> none  [the longest x2 19.3 us: on_device(): lax.all_to_all(spectra, 'tm', split_axis=3, concat_axis=1, tiled=True)]
    all_to_all x0 -> x1, waiting for transfers between devices: none -> 16 us  [on_device(): lax.all_to_all(pieces, 'tm', 0, 0, axis_index_groups=groups, tiled=True)]
  transfers between devices with their start and end apart: 2 -> 3, of which waited for: 2 -> 3; matrix products, arithmetic and copies ran while one was open for 1% -> 2% of each run, Pallas kernels for 0% -> 0%
where the time goes in v1:
time: 192 us; the launch traced here: 191 us
  blocking collectives  73.7 us (38%)
  waiting for transfers between devices  42.9 us (22%)
  Pallas kernels  31 us (16%)
  between operations  17.5 us (9%)
  starting transfers between devices  14.9 us (8%)
  local copies, waits for them, and re-layouts  7.53 us (4%)
  other arithmetic  3.65 us (2%)
    all_to_all x1, blocking collectives, on_device(): moved = lax.all_to_all(chunks, ('tm', 'ct'), 0, 0, tiled=True)  73.7 us
    pallas_call x1, Pallas kernels, correlated(): pl.pallas_call(correlate_kernel, out_shape=jax.ShapeDtypeStruct((2, SLOW,...  18.2 us
    all_to_all x1, waiting for transfers between devices, on_device(): lax.all_to_all(pieces, 'tm', 0, 0, axis_index_groups=groups, tiled=True)  16 us
    all_gather x1, waiting for transfers between devices, on_device(): return correlated(lax.all_gather(moved, 'stn', axis=0))  15.5 us
    pallas_call x1, Pallas kernels, spectra_of(): pl.pallas_call(spectra_kernel, out_shape=jax.ShapeDtypeStruct((FAST, 2, 2...  12.8 us
    ppermute x1, waiting for transfers between devices, on_device(): lax.ppermute(own[GROUP - 1], 'tm', [(t, t + GROUP) for t in range(28)])  11.4 us
    ppermute x1, starting transfers between devices, on_device(): lax.ppermute(own[GROUP - 1], 'tm', [(t, t + GROUP) for t in range(28)])  9.71 us
    all_to_all x1, starting transfers between devices, on_device(): lax.all_to_all(pieces, 'tm', 0, 0, axis_index_groups=groups, tiled=True)  5.14 us
  transfers between devices with their start and end apart: 3, of which 3 were waited for; matrix products, arithmetic and copies ran while one was open for 2% of the time, Pallas kernels for 0%

profile of v1, /device:TPU:1, one launch (start us, length us, event | category | flops | bytes accessed | tf_op | source)
XLA Modules:
  0.0 191.2 jit_solution(14150134271341544091)
XLA Ops:
  6.5 2.7 %copy.15 = bf16[2,8,16,4096]{3,2,1,0:T(8,128)(2,1)S(1)} copy(bf16[2,8,16,4096]{3,1,2,0:T(8,128)(2,1)} %bitcast.47) | data formatting | bytes 4194304
  9.3 1.6 copy.19
  10.8 0.0 copy-start.2
  10.9 0.0 copy-start.1
  10.9 5.1 %all-to-all-start = ((bf16[4,2,2,16,4096]{4,3,2,1,0:T(8,128)(2,1)}), bf16[4,2,2,16,4096]{4,3,2,1,0:T(8,128)(2,1)S(1)}, u32[]{:S(2)}, u32[]{:S(2)}) async-start(bf16[4,2,2,16,4096]{4,3,2,1,0:T(8,128)(2,1)} %bitcast.45), calls=%async_computation | async-start | bytes 4194304 | tf_op jit(solution)/shard_map/all_to_all | solution.py:235
  16.0 0.0 all-gather.3.cloned.1.call-start
  16.0 0.0 copy-done.2
  16.0 0.1 dynamic_slice.9
  16.1 0.7 fusion.32
  19.4 0.6 iota_add_fusion.1
  20.1 0.7 iota_add_fusion
  20.8 0.7 add_compare_fusion
  21.5 0.7 add_compare_fusion.1
  23.5 0.1 fusion.29
  23.6 0.1 fusion.31
  23.6 0.3 fusion.15
  23.9 0.3 fusion.13
  24.2 0.0 copy-done.1
  24.2 0.2 constant_dynamic-slice_fusion.1
  24.4 0.1 select_bitcast_fusion
  24.6 16.0 %all-to-all-done.own_ref = bf16[4,2,2,16,4096]{4,3,2,1,0:T(8,128)(2,1)S(1)} async-done(((bf16[4,2,2,16,4096]{4,3,2,1,0:T(8,128)(2,1)}), bf16[4,2,2,16,4096]{4,3,2,1,0:T(8,128)(2,1)S(1)}, u32[]{:S(2)}, u32[]{:S(2)}) %all-to-all-start) | async-done | bytes 2097184 | tf_op jit(solution)/shard_map/all_to_all | solution.py:235
  40.6 9.7 %collective-permute-start = (bf16[2,2,16,4096]{3,2,1,0:T(8,128)(2,1)S(1)}, bf16[2,2,16,4096]{3,2,1,0:T(8,128)(2,1)S(1)}, u32[]{:S(2)}, u32[]{:S(2)}) collective-permute-start(bf16[2,2,16,4096]{3,2,1,0:T(8,128)(2,1)S(1)} %slice_bitcast_fusion), channel_id=1, source_target_pairs={{0,16},{4,20},{8,24},{12,28},{16,32},{20,36},{24,40},{28,44},{32,4... | collective-permute-start | bytes 1572872 | tf_op jit(solution)/shard_map/ppermute | solution.py:236
  50.5 0.1 pad_maximum_fusion.taps_ref
  50.5 11.4 %collective-permute-done.halo_ref = bf16[2,2,16,4096]{3,2,1,0:T(8,128)(2,1)S(1)} collective-permute-done((bf16[2,2,16,4096]{3,2,1,0:T(8,128)(2,1)S(1)}, bf16[2,2,16,4096]{3,2,1,0:T(8,128)(2,1)S(1)}, u32[]{:S(2)}, u32[]{:S(2)}) %collective-permute-start) | collective-permute-done | bytes 524320 | tf_op jit(solution)/shard_map/ppermute | solution.py:236
  61.9 12.8 %shard_map.46 = bf16[128,2,2,16,128]{4,3,2,1,0:T(8,128)(2,1)S(1)} custom-call(bf16[4,2,2,16,4096]{4,3,2,1,0:T(8,128)(2,1)S(1)} %all-to-all-done.own_ref, bf16[2,2,16,4096]{3,2,1,0:T(8,128)(2,1)S(1)} %collective-permute-done.halo_ref, f32[2,32,24,128]{3,2,1,0:T(8,128)S(1)} %pad_maximum_fusion.taps_ref, f32[2,2,32,128]{3,2,1,0:T(8,128)S(1)} %pad_maximum_fusion.1.turn_ref, ...), custom_call_target="tpu_custom_call" | custom-call | tf_op jit(solution)/shard_map/pallas_call | solution.py:143
  74.8 73.7 %all_to_all.10 = bf16[128,2,2,16,128]{4,3,2,1,0:T(8,128)(2,1)} all-to-all(bf16[128,2,2,16,128]{4,3,2,1,0:T(8,128)(2,1)S(1)} %shard_map.46), channel_id=1, replica_groups=mesh['stn'=2,'tm'=32,'ct'=4] {'tm','ct'}, dimensions={0} | all-to-all | bytes 4194304 | tf_op jit(solution)/shard_map/all_to_all | solution.py:238
  148.4 0.0 all-gather.3.cloned.1.call-update
  148.5 15.5 %all-gather.3.cloned.1.call-done = bf16[256,2,2,16,128]{4,3,2,1,0:T(8,128)(2,1)} async-done(((bf16[128,2,2,16,128]{4,3,2,1,0:T(8,128)(2,1)}), bf16[256,2,2,16,128]{4,3,2,1,0:T(8,128)(2,1)}) %all-gather.3.cloned.1.call-update) | async-done | bytes 4194320 | tf_op jit(solution)/shard_map/all_gather | solution.py:239
  164.0 0.0 copy-start
  164.0 2.2 %copy-done = bf16[256,2,2,16,128]{4,3,2,1,0:T(8,128)(2,1)S(1)} copy-done((bf16[256,2,2,16,128]{4,3,2,1,0:T(8,128)(2,1)S(1)}, bf16[256,2,2,16,128]{4,3,2,1,0:T(8,128)(2,1)}, u32[]{:S(2)}) %copy-start) | copy-done | bytes 4194328
  166.1 18.2 %shard_map.47 = f32[2,32,32,64]{3,2,1,0:T(8,128)} custom-call(bf16[2,128,2,2,16,128]{5,4,3,2,1,0:T(8,128)(2,1)S(1)} %bitcast.44), custom_call_target="tpu_custom_call" | custom-call | tf_op jit(solution)/shard_map/pallas_call | solution.py:214
  (7 shorter events, 0.2 us)
Async XLA Ops:
  10.8 5.2 %copy-start.2 = (s32[8]{0:T(128)S(1)}, s32[8]{0:T(128)}, u32[]{:S(2)}) copy-start(s32[8]{0:T(128)} %param.5) | copy-start | bytes 100
  10.9 13.4 %copy-start.1 = (f32[16,8192]{1,0:T(8,128)S(1)}, f32[16,8192]{1,0:T(8,128)}, u32[]{:S(2)}) copy-start(f32[16,8192]{1,0:T(8,128)} %constant.73.clone) | copy-start | bytes 1572868
  10.9 29.7 %all-to-all-start = ((bf16[4,2,2,16,4096]{4,3,2,1,0:T(8,128)(2,1)}), bf16[4,2,2,16,4096]{4,3,2,1,0:T(8,128)(2,1)S(1)}, u32[]{:S(2)}, u32[]{:S(2)}) async-start(bf16[4,2,2,16,4096]{4,3,2,1,0:T(8,128)(2,1)} %bitcast.45), calls=%async_computation | async-start | bytes 4194304 | tf_op jit(solution)/shard_map/all_to_all | solution.py:235
  16.0 148.0 %all-gather.3.cloned.1.call-start = ((), (), s32[]{:S(2)}) async-start(), calls=%async_computation.2 | async-start | bytes 6291456 | tf_op jit(solution)/shard_map/all_gather | solution.py:239
  40.6 21.3 %collective-permute-start = (bf16[2,2,16,4096]{3,2,1,0:T(8,128)(2,1)S(1)}, bf16[2,2,16,4096]{3,2,1,0:T(8,128)(2,1)S(1)}, u32[]{:S(2)}, u32[]{:S(2)}) collective-permute-start(bf16[2,2,16,4096]{3,2,1,0:T(8,128)(2,1)S(1)} %slice_bitcast_fusion), channel_id=1, source_target_pairs={{0,16},{4,20},{8,24},{12,28},{16,32},{20,36},{24,40},{28,44},{32,4... | collective-permute-start | bytes 1572872 | tf_op jit(solution)/shard_map/ppermute | solution.py:236
  164.0 2.2 %copy-start = (bf16[256,2,2,16,128]{4,3,2,1,0:T(8,128)(2,1)S(1)}, bf16[256,2,2,16,128]{4,3,2,1,0:T(8,128)(2,1)}, u32[]{:S(2)}) copy-start(bf16[256,2,2,16,128]{4,3,2,1,0:T(8,128)(2,1)} %all-gather.3.cloned.1.call-done) | copy-start | bytes 12582916
Sparse Core Ops, SparseCore 0:
  148.6 15.3 all-gather.2

commit v2 on v1

v2 whole, which is shorter than its diff:
```python
import math

import jax
import jax.numpy as jnp
import numpy as np
from jax import lax
from jax.experimental import pallas as pl
from jax.experimental.pallas import tpu as pltpu
from jax.sharding import PartitionSpec as P

CHANNELS = 4096
TAPS = 16
SLOW = 32
FAST = 128
BLOCK = 16
GROUP = 4
FRAMES = 512
OWNERS = 128
MESH = pl.DeviceIdType.MESH


def filter_table():
    length = TAPS * CHANNELS
    index = np.arange(length, dtype=np.float64)
    centred = (index - length / 2) / CHANNELS
    window = 0.5 - 0.5 * np.cos(2.0 * math.pi * index / length)
    factor = 1.0 / (48.0 * math.sqrt(CHANNELS))
    return (np.sinc(centred) * window * factor).reshape(TAPS, CHANNELS).astype(np.float32)


def rolled_filter(delay):
    table = filter_table()
    doubled = jnp.asarray(np.concatenate([table, table], axis=1))
    turned = lax.dynamic_slice(doubled, (0, delay), (TAPS, CHANNELS))
    carry = jnp.arange(CHANNELS, dtype=jnp.int32) + delay >= CHANNELS
    later = jnp.pad(turned, ((1, 7), (0, 0)))
    same = jnp.pad(turned, ((0, 8), (0, 0)))
    taps = jnp.where(carry[None, :], later, same)
    return taps.reshape(24, SLOW, FAST).transpose(1, 0, 2)


def turn_tables(delay):
    k = jnp.arange(SLOW, dtype=jnp.int32)[:, None]
    q = jnp.arange(FAST, dtype=jnp.int32)[None, :]
    angle = (k * (q + delay) % CHANNELS).astype(jnp.float32) * (2.0 * math.pi / CHANNELS)
    return jnp.stack([jnp.cos(angle), jnp.sin(angle)])


def last_table(delay):
    l = jnp.arange(FAST, dtype=jnp.int32)[:, None]
    q = jnp.arange(FAST, dtype=jnp.int32)[None, :]
    angle = (l * (q + delay) % FAST).astype(jnp.float32) * (2.0 * math.pi / FAST)
    cosine, sine = jnp.cos(angle), jnp.sin(angle)
    upper = jnp.concatenate([cosine, sine], axis=1)
    lower = jnp.concatenate([-sine, cosine], axis=1)
    return jnp.concatenate([upper, lower], axis=0).astype(jnp.bfloat16)


def fft(xs):
    n = len(xs)
    if n == 1:
        return xs
    even, odd = fft(xs[0::2]), fft(xs[1::2])
    low, high = [], []
    for k in range(n // 2):
        re, im = odd[k]
        if k == 0:
            tr, ti = re, im
        elif 4 * k == n:
            tr, ti = im, -re
        elif 8 * k == n:
            s = math.sqrt(0.5)
            tr, ti = (re + im) * s, (im - re) * s
        elif 8 * k == 3 * n:
            s = math.sqrt(0.5)
            tr, ti = (im - re) * s, (im + re) * (-s)
        else:
            c, s = math.cos(2 * math.pi * k / n), math.sin(2 * math.pi * k / n)
            tr, ti = re * c + im * s, im * c - re * s
        er, ei = even[k]
        low.append((er + tr, ei + ti))
        high.append((er - tr, ei - ti))
    return low + high


def filter_and_transform(i, own, halo, taps_ref, turn_ref, last_ref, xs, branch, inner, flat):
    @pl.loop(0, SLOW)
    def _(b):
        lanes = pl.ds(pl.multiple_of(b * FAST, FAST), FAST)
        taps = [jnp.broadcast_to(taps_ref[i, b, k : k + 1, :], (8, FAST)) for k in range(TAPS + 1)]
        for r in range(2):
            xs[r, 0:BLOCK, :] = halo[i, r, :, lanes].astype(jnp.float32)
            for g in range(GROUP):
                first = BLOCK * (g + 1)
                xs[r, first : first + BLOCK, :] = own[g, i, r, :, lanes].astype(jnp.float32)
        for r in range(2):
            total = [None] * 8
            for s in range(-16, 57):
                window = xs[r, BLOCK + s : BLOCK + s + 8, :]
                for o in range(8):
                    k = 8 * o - s
                    if 0 <= k <= TAPS:
                        term = taps[k] * window
                        total[o] = term if total[o] is None else total[o] + term
                    if k == 0:
                        branch[r, b, 8 * o : 8 * o + 8, :] = total[o]

    @pl.loop(0, 8)
    def _(o):
        rows = pl.ds(pl.multiple_of(o * 8, 8), 8)
        points = [(branch[0, b, rows, :], branch[1, b, rows, :]) for b in range(SLOW)]
        for k, (re, im) in enumerate(fft(points)):
            c = jnp.broadcast_to(turn_ref[i, 0, k : k + 1, :], (8, FAST))
            s = jnp.broadcast_to(turn_ref[i, 1, k : k + 1, :], (8, FAST))
            inner[k, rows, 0:FAST] = re * c + im * s
            inner[k, rows, FAST : 2 * FAST] = im * c - re * s

    @pl.loop(0, 8)
    def _(g):
        points = inner[pl.ds(g * 4, 4), :, :].reshape(4 * 64, 2 * FAST).astype(jnp.bfloat16)
        result = lax.dot_general(
            last_ref[i], points, (((1,), (1,)), ((), ())), preferred_element_type=jnp.float32
        )
        for r in range(2):
            for t in range(2):
                for l in range(16):
                    piece = result[r * FAST + 8 * l : r * FAST + 8 * l + 8, t * FAST : t * FAST + FAST]
                    flat[r, pl.ds(l * 128 + g * 2 + t, 8, stride=16), :] = piece


def gather_pair(pair, got, wide, packed):
    low = lax.broadcasted_iota(jnp.int32, (8, FAST), 1) < 64

    @pl.loop(0, 4)
    def _(step):
        t = step // 2
        stn = step % 2
        for ct in range(4):
            for y in range(4):
                for i in range(2):
                    for r in range(2):
                        row = stn * 32 + (ct * 4 + y) * 2 + i
                        source = (pair * 2 + t) * 16 + y * 4 + ct
                        place = pl.ds(pl.multiple_of(row * 16, 16), 16)
                        wide[t, r, place, :] = got[stn, source, i, r, :, :].astype(jnp.float32)

    lanes = pl.ds(pl.multiple_of(pair * FAST, FAST), FAST)

    def reorder(j):
        for r in range(2):
            for g in range(4):
                even, odd = [], []
                for h in range(2):
                    rows = pl.ds((g * 16 + h * 8) * 16 + j, 8, stride=16)
                    a, b = wide[0, r, rows, :], wide[1, r, rows, :]
                    crossed = pltpu.roll(jnp.where(low, b, a), 64, 1)
                    even.append(jnp.where(low, a, crossed))
                    odd.append(jnp.where(low, crossed, b))
                place = slice(r * 64 + g * 16, r * 64 + g * 16 + 16)
                packed[2 * j, place, lanes] = jnp.concatenate(even, axis=0).astype(jnp.bfloat16)
                packed[2 * j + 1, place, lanes] = jnp.concatenate(odd, axis=0).astype(jnp.bfloat16)

    @pl.loop(0, 16, step=4)
    def _(j0):
        for u in range(4):
            reorder(j0 + u)


def correlate(mine, packed, out_ref):
    @pl.loop(0, SLOW, step=4)
    def _(k0):
        for u in range(4):
            k = k0 + u
            left = jnp.concatenate(
                [packed[k, pl.ds(pl.multiple_of(r * 64 + mine * 32, 32), 32), :] for r in range(2)],
                axis=0,
            )
            grid = lax.dot_general(
                left, packed[k], (((1,), (1,)), ((), ())), preferred_element_type=jnp.float32
            )
            out_ref[0, k, :, :] = (grid[0:32, 0:64] + grid[32:64, 64:128]) * (1.0 / FRAMES)
            out_ref[1, k, :, :] = (grid[32:64, 0:64] - grid[0:32, 64:128]) * (1.0 / FRAMES)


def whole_kernel(
    pieces,
    taps_ref,
    turn_ref,
    last_ref,
    out_ref,
    own,
    halo,
    chunks,
    got,
    xs,
    branch,
    inner,
    flat,
    wide,
    packed,
    near_send,
    near_recv,
    halo_send,
    halo_recv,
    far_send,
    far_recv,
    twin_send,
    twin_recv,
):
    tm, ct, stn = lax.axis_index("tm"), lax.axis_index("ct"), lax.axis_index("stn")
    me = tm * 4 + ct
    y, block, column = tm % 4, tm // 4, tm // 8

    barrier = pltpu.get_barrier_semaphore()

    @pl.loop(1, OWNERS)
    def _(j):
        l = (me + j) % OWNERS
        pl.semaphore_signal(
            barrier, inc=1, device_id={"tm": l // 4, "ct": l % 4}, device_id_type=MESH
        )

    pl.semaphore_signal(barrier, inc=1, device_id={"stn": 1 - stn}, device_id_type=MESH)

    @pl.when(block == 0)
    def _():
        halo[...] = jnp.zeros_like(halo)

    pl.semaphore_wait(barrier, OWNERS)

    def near(i, offset):
        other = (y + offset) % GROUP
        return pltpu.make_async_remote_copy(
            src_ref=pieces.at[other, i],
            dst_ref=own.at[y, i],
            send_sem=near_send.at[i, offset],
            recv_sem=near_recv.at[i, y],
            device_id={"tm": block * 4 + other},
            device_id_type=MESH,
        )

    def near_arrival(i, source):
        return pltpu.make_async_copy(pieces.at[0, i], own.at[source, i], near_recv.at[i, source])

    def halo_copy(i):
        return pltpu.make_async_remote_copy(
            src_ref=own.at[GROUP - 1, i],
            dst_ref=halo.at[i],
            send_sem=halo_send.at[i],
            recv_sem=halo_recv.at[i],
            device_id={"tm": (tm + GROUP) % 32},
            device_id_type=MESH,
        )

    for i in range(2):
        pltpu.make_async_copy(pieces.at[y, i], own.at[y, i], near_recv.at[i, y]).start()
        for offset in (1, 3, 2):
            near(i, offset).start()
    for i in range(2):
        near_arrival(i, GROUP - 1).wait()

        @pl.when(block < 7)
        def _():
            halo_copy(i).start()

    def far(l, i):
        return pltpu.make_async_remote_copy(
            src_ref=chunks.at[l, i],
            dst_ref=got.at[stn, me, i],
            send_sem=far_send,
            recv_sem=far_recv.at[column],
            device_id={"tm": l // 4, "ct": l % 4},
            device_id_type=MESH,
        )

    @pl.loop(0, 2)
    def _(i):
        for source in range(GROUP - 1):
            near_arrival(i, source).wait()

        @pl.when(block > 0)
        def _():
            halo_copy(i).wait_recv()

        filter_and_transform(i, own, halo, taps_ref, turn_ref, last_ref, xs, branch, inner, flat)

        @pl.loop(0, OWNERS, step=4)
        def _(j0):
            for u in range(4):
                l = (me + j0 + u) % OWNERS
                rows = pl.ds(pl.multiple_of(l * 16, 16), 16)
                for r in range(2):
                    chunks[l, i, r, :, :] = flat[r, rows, :].astype(jnp.bfloat16)

            @pl.when(j0 == 0)
            def _():
                pltpu.make_async_copy(
                    chunks.at[me, i], got.at[stn, me, i], far_recv.at[column]
                ).start()

            @pl.when(j0 > 0)
            def _():
                far((me + j0) % OWNERS, i).start()

            for u in range(1, 4):
                far((me + j0 + u) % OWNERS, i).start()

    def twin(p):
        rows = got.at[stn, pl.ds(p * 32, 32)]
        return pltpu.make_async_remote_copy(
            src_ref=rows,
            dst_ref=rows,
            send_sem=twin_send.at[p],
            recv_sem=twin_recv.at[p],
            device_id={"stn": 1 - stn},
            device_id_type=MESH,
        )

    def hand_over(p):
        rows = got.at[stn, pl.ds(p * 32, 32)]
        pltpu.make_async_copy(rows, rows, far_recv.at[p]).wait()
        twin(p).start()

    hand_over((column + 3) % 4)

    @pl.loop(0, 4)
    def _(step):
        p = (column + 3 - step) % 4

        @pl.when(step < 3)
        def _():
            hand_over((column + 2 - step + 4) % 4)

        twin(p).wait_recv()
        gather_pair(p, got, wide, packed)

    correlate(stn, packed, out_ref)

    for i in range(2):
        for offset in (1, 3, 2):
            near(i, offset).wait_send()

        @pl.when(block < 7)
        def _():
            halo_copy(i).wait_send()

    for p in range(4):
        twin(p).wait_send()
    sent = chunks.at[pl.ds(0, OWNERS - 1)]
    pltpu.make_async_copy(sent, sent, far_send).wait()


def on_device(voltages, delays):
    where = lax.axis_index("tm") % GROUP
    mine = lax.dynamic_slice(delays, (2 * where,), (2,))
    taps = jnp.stack([rolled_filter(mine[i]) for i in range(2)])
    turn = jnp.stack([turn_tables(mine[i]) for i in range(2)])
    last = jnp.stack([last_table(mine[i]) for i in range(2)])
    pieces = voltages.reshape(2, GROUP, 2, BLOCK, CHANNELS).transpose(1, 2, 0, 3, 4)
    dma = pltpu.SemaphoreType.DMA
    f32, bf16 = jnp.float32, jnp.bfloat16
    return pl.pallas_call(
        whole_kernel,
        out_shape=jax.ShapeDtypeStruct((2, SLOW, 32, 64), f32),
        in_specs=[pl.BlockSpec(memory_space=pltpu.VMEM)] * 4,
        out_specs=pl.BlockSpec(memory_space=pltpu.VMEM),
        scratch_shapes=[
            pltpu.VMEM((GROUP, 2, 2, BLOCK, CHANNELS), bf16),
            pltpu.VMEM((2, 2, BLOCK, CHANNELS), bf16),
            pltpu.VMEM((OWNERS, 2, 2, 16, FAST), bf16),
            pltpu.VMEM((2, OWNERS, 2, 2, 16, FAST), bf16),
            pltpu.VMEM((2, 80, FAST), f32),
            pltpu.VMEM((2, SLOW, 64, FAST), f32),
            pltpu.VMEM((SLOW, 64, 2 * FAST), f32),
            pltpu.VMEM((2, FAST * 16, FAST), f32),
            pltpu.VMEM((2, 2, 64 * 16, FAST), f32),
            pltpu.VMEM((SLOW, FAST, 4 * FAST), bf16),
            dma((2, GROUP)),
            dma((2, GROUP)),
            dma((2,)),
            dma((2,)),
            dma,
            dma((4,)),
            dma((4,)),
            dma((4,)),
        ],
        compiler_params=pltpu.CompilerParams(
            collective_id=0, has_side_effects=True, vmem_limit_bytes=56 << 20
        ),
    )(pieces, taps, turn, last)


def solution(mesh):
    return jax.shard_map(
        on_device,
        mesh=mesh,
        in_specs=(P(None, ("stn", "ct"), "tm"), P(("stn", "ct"))),
        out_specs=P(None, ("tm", "ct"), "stn", None),
        check_vma=False,
    )
```

time: 192 us -> 124 us (0.65)
  Pallas kernels: 31 us -> 106 us
  blocking collectives: 73.7 us -> 0 us
  waiting for transfers between devices: 42.9 us -> 0 us
  starting transfers between devices: 14.9 us -> 0 us
  between operations: 17.5 us -> 4.17 us
  other arithmetic: 3.65 us -> 5.87 us
    pallas_call x2 -> x1, Pallas kernels: 31 us -> 106 us  [on_device(): pl.pallas_call(whole_kernel, out_shape=jax.ShapeDtypeStruct((2, SLOW, 32,...]
    all_to_all x1 -> x0, blocking collectives: 73.7 us -> none  [on_device(): moved = lax.all_to_all(chunks, ('tm', 'ct'), 0, 0, tiled=True)]
    all_to_all x1 -> x0, waiting for transfers between devices: 16 us -> none  [on_device(): lax.all_to_all(pieces, 'tm', 0, 0, axis_index_groups=groups, tiled=True)]
    all_gather x1 -> x0, waiting for transfers between devices: 15.5 us -> none  [on_device(): return correlated(lax.all_gather(moved, 'stn', axis=0))]
    ppermute x1 -> x0, waiting for transfers between devices: 11.4 us -> none  [on_device(): lax.ppermute(own[GROUP - 1], 'tm', [(t, t + GROUP) for t in range(28)])]
    ppermute x1 -> x0, starting transfers between devices: 9.71 us -> none  [on_device(): lax.ppermute(own[GROUP - 1], 'tm', [(t, t + GROUP) for t in range(28)])]
    all_to_all x1 -> x0, starting transfers between devices: 5.14 us -> none  [on_device(): lax.all_to_all(pieces, 'tm', 0, 0, axis_index_groups=groups, tiled=True)]
    unnamed x7 -> x6, local copies, waits for them, and re-layouts: 4.94 us -> 5.02 us
  transfers between devices with their start and end apart: 3 -> 0, of which waited for: 3 -> 0; matrix products, arithmetic and copies ran while one was open for 2% -> 0% of each run, Pallas kernels for 0% -> 0%
where the time goes in v2:
time: 124 us; the launch traced here: 123 us
  Pallas kernels  106 us (85%)
  local copies, waits for them, and re-layouts  7.47 us (6%)
  other arithmetic  5.87 us (5%)
  between operations  4.17 us (3%)
    pallas_call x1, Pallas kernels, on_device(): pl.pallas_call(whole_kernel, out_shape=jax.ShapeDtypeStruct((2, SLOW, 32,...  106 us
    unnamed x6, local copies, waits for them, and re-layouts  5.02 us

profile of v2, /device:TPU:1, one launch (start us, length us, event | category | flops | bytes accessed | tf_op | source)
XLA Modules:
  0.0 123.3 jit_solution(2344598603277475433)
XLA Ops:
  0.0 2.7 %copy.12 = bf16[2,8,16,4096]{3,2,1,0:T(8,128)(2,1)S(1)} copy(bf16[2,8,16,4096]{3,1,2,0:T(8,128)(2,1)} %bitcast.43) | data formatting | bytes 4194304
  2.7 0.0 copy-start.1
  2.8 0.0 copy-start
  2.8 1.5 %copy.16 = bf16[2,4,2,16,4096]{4,3,0,2,1:T(8,128)(2,1)} copy(bf16[2,4,2,16,4096]{4,3,2,1,0:T(8,128)(2,1)S(1)} %bitcast.42) | data formatting | bytes 4194304 | tf_op jit(solution)/shard_map/reshape | solution.py:359
  4.2 0.0 copy-done.1
  4.2 0.1 dynamic_slice.9
  4.3 0.7 fusion.32
  9.0 0.0 copy-done
  9.0 0.2 constant_dynamic-slice_fusion.1
  9.2 0.7 add_compare_fusion
  9.9 0.7 add_compare_fusion.1
  10.6 0.1 select_bitcast_fusion
  10.8 0.9 pad_maximum_fusion.taps_ref
  11.7 0.7 iota_add_fusion.1
  12.4 0.1 fusion.31
  12.5 0.7 iota_add_fusion
  13.2 0.1 fusion.29
  13.3 0.6 pad_maximum_fusion.1.turn_ref
  13.9 0.3 fusion.15
  14.2 0.3 fusion.13
  14.5 0.7 maximum_maximum_fusion.last_ref
  15.2 105.8 %shard_map.46 = f32[2,32,32,64]{3,2,1,0:T(8,128)} custom-call(bf16[4,2,2,16,4096]{4,3,2,1,0:T(8,128)(2,1)} %bitcast.41, f32[2,32,24,128]{3,2,1,0:T(8,128)} %pad_maximum_fusion.taps_ref, f32[2,2,32,128]{3,2,1,0:T(8,128)} %pad_maximum_fusion.1.turn_ref, bf16[2,256,256]{2,1,0:T(8,128)(2,1)} %maximum_maximum_fusion.last_ref), custom_call_target="tpu_custom_call" | custom-call | tf_op jit(solution)/shard_map/pallas_call | solution.py:362
  121.0 2.3 %copy.20 = f32[2,32,32,64]{3,2,1,0:T(8,128)} copy(f32[2,32,32,64]{3,2,1,0:T(8,128)} %shard_map.46) | data formatting | bytes 1048576
  (4 shorter events, 0.1 us)
Async XLA Ops:
  2.7 1.5 %copy-start.1 = (s32[8]{0:T(128)S(1)}, s32[8]{0:T(128)}, u32[]{:S(2)}) copy-start(s32[8]{0:T(128)} %param.5) | copy-start | bytes 100
  2.8 6.3 %copy-start = (f32[16,8192]{1,0:T(8,128)S(1)}, f32[16,8192]{1,0:T(8,128)}, u32[]{:S(2)}) copy-start(f32[16,8192]{1,0:T(8,128)} %constant.73.clone) | copy-start | bytes 1572868

commit v3 on v2

--- a/solution.py
+++ b/solution.py
@@ -28,32 +28,23 @@
     return (np.sinc(centred) * window * factor).reshape(TAPS, CHANNELS).astype(np.float32)
 
 
-def rolled_filter(delay):
-    table = filter_table()
-    doubled = jnp.asarray(np.concatenate([table, table], axis=1))
-    turned = lax.dynamic_slice(doubled, (0, delay), (TAPS, CHANNELS))
-    carry = jnp.arange(CHANNELS, dtype=jnp.int32) + delay >= CHANNELS
-    later = jnp.pad(turned, ((1, 7), (0, 0)))
-    same = jnp.pad(turned, ((0, 8), (0, 0)))
-    taps = jnp.where(carry[None, :], later, same)
-    return taps.reshape(24, SLOW, FAST).transpose(1, 0, 2)
-
-
-def turn_tables(delay):
-    k = jnp.arange(SLOW, dtype=jnp.int32)[:, None]
-    q = jnp.arange(FAST, dtype=jnp.int32)[None, :]
-    angle = (k * (q + delay) % CHANNELS).astype(jnp.float32) * (2.0 * math.pi / CHANNELS)
-    return jnp.stack([jnp.cos(angle), jnp.sin(angle)])
-
-
-def last_table(delay):
-    l = jnp.arange(FAST, dtype=jnp.int32)[:, None]
-    q = jnp.arange(FAST, dtype=jnp.int32)[None, :]
-    angle = (l * (q + delay) % FAST).astype(jnp.float32) * (2.0 * math.pi / FAST)
-    cosine, sine = jnp.cos(angle), jnp.sin(angle)
-    upper = jnp.concatenate([cosine, sine], axis=1)
-    lower = jnp.concatenate([-sine, cosine], axis=1)
-    return jnp.concatenate([upper, lower], axis=0).astype(jnp.bfloat16)
+def tap_blocks():
+    return filter_table().reshape(TAPS, SLOW, FAST).transpose(1, 0, 2)
+
+
+def turn_blocks():
+    angle = np.arange(SLOW)[:, None] * np.arange(CHANNELS)[None, :] % CHANNELS
+    angle = angle * (2.0 * math.pi / CHANNELS)
+    both = np.concatenate([np.cos(angle), np.sin(angle)]).astype(np.float32)
+    return both.reshape(2 * SLOW, SLOW, FAST).transpose(1, 0, 2)
+
+
+def last_table():
+    angle = np.arange(FAST)[:, None] * np.arange(FAST)[None, :] % FAST * (2.0 * math.pi / FAST)
+    cosine, sine = np.cos(angle), np.sin(angle)
+    upper = np.concatenate([cosine, sine], axis=1)
+    lower = np.concatenate([-sine, cosine], axis=1)
+    return np.concatenate([upper, lower], axis=0).astype(np.float32)
 
 
 def fft(xs):
@@ -83,38 +74,92 @@
     return low + high
 
 
-def filter_and_transform(i, own, halo, taps_ref, turn_ref, last_ref, xs, branch, inner, flat):
+def split_inputs(voltages, spread, pieces):
+    @pl.loop(0, SLOW)
+    def _(b):
+        lanes = pl.ds(pl.multiple_of(b * FAST, FAST), FAST)
+        for r in range(2):
+            for f in range(BLOCK):
+                there = pl.ds(pl.multiple_of(f * CHANNELS + b * FAST, FAST), FAST)
+                spread[r, pl.ds(f, 8, stride=BLOCK), :] = voltages[r, :, there].astype(jnp.float32)
+        for r in range(2):
+            for i in range(8):
+                rows = spread[r, BLOCK * i : BLOCK * i + BLOCK, :]
+                pieces[i // 2, i % 2, r, :, lanes] = rows.astype(jnp.bfloat16)
+
+
+def delayed_tables(i, delay, tap_ref, turn_all, last_all, taps_ref, turn_ref, last_ref):
+    high, low = delay >> 7, delay & 127
+    lane = lax.broadcasted_iota(jnp.int32, (1, FAST), 1)
+    same = lane < FAST - low
+    shift = (FAST - low) & 127
+
+    def ahead(table, b):
+        first = pltpu.roll(table[(b + high) & 31], shift, 1)
+        second = pltpu.roll(table[(b + high + 1) & 31], shift, 1)
+        return jnp.where(same, first, second)
+
+    @pl.loop(0, SLOW)
+    def _(b):
+        rolled = ahead(tap_ref, b)
+        carry = lane + b * FAST + delay >= CHANNELS
+        taps_ref[i, b, 0:TAPS, :] = jnp.where(carry, 0.0, rolled)
+        taps_ref[i, b, TAPS : TAPS + 8, :] = jnp.zeros((8, FAST), jnp.float32)
+        taps_ref[i, b, 1 : TAPS + 1, :] += jnp.where(carry, rolled, 0.0)
+
+    turn_ref[i] = ahead(turn_all, 0)
+
+    @pl.loop(0, 8)
+    def _(g):
+        rows = pl.ds(pl.multiple_of(g * 32, 32), 32)
+        for part in range(2):
+            lanes = slice(part * FAST, part * FAST + FAST)
+            last_ref[i, rows, lanes] = pltpu.roll(last_all[rows, lanes], shift, 1).astype(jnp.bfloat16)
+
+
+def filter_frames(i, own, halo, taps_ref, xs, branch, first):
+    octets = range(2) if first else range(2, 8)
+    base = BLOCK if first else 0
+
     @pl.loop(0, SLOW)
     def _(b):
         lanes = pl.ds(pl.multiple_of(b * FAST, FAST), FAST)
         taps = [jnp.broadcast_to(taps_ref[i, b, k : k + 1, :], (8, FAST)) for k in range(TAPS + 1)]
         for r in range(2):
-            xs[r, 0:BLOCK, :] = halo[i, r, :, lanes].astype(jnp.float32)
-            for g in range(GROUP):
-                first = BLOCK * (g + 1)
-                xs[r, first : first + BLOCK, :] = own[g, i, r, :, lanes].astype(jnp.float32)
-        for r in range(2):
-            total = [None] * 8
-            for s in range(-16, 57):
-                window = xs[r, BLOCK + s : BLOCK + s + 8, :]
-                for o in range(8):
+            if first:
+                xs[r, 0:BLOCK, :] = halo[i, r, :, lanes].astype(jnp.float32)
+                xs[r, BLOCK : 2 * BLOCK, :] = own[0, i, r, :, lanes].astype(jnp.float32)
+            else:
+                for g in range(GROUP):
+                    xs[r, BLOCK * g : BLOCK * g + BLOCK, :] = own[g, i, r, :, lanes].astype(
+                        jnp.float32
+                    )
+        for r in range(2):
+            total = {}
+            for s in range(8 * octets[0] - TAPS, 8 * octets[-1] + 1):
+                window = xs[r, base + s : base + s + 8, :]
+                for o in octets:
                     k = 8 * o - s
                     if 0 <= k <= TAPS:
                         term = taps[k] * window
-                        total[o] = term if total[o] is None else total[o] + term
+                        total[o] = total[o] + term if o in total else term
                     if k == 0:
                         branch[r, b, 8 * o : 8 * o + 8, :] = total[o]
 
-    @pl.loop(0, 8)
+
+def slow_transform(i, turn_ref, branch, inner, first):
+    @pl.loop(*((0, 2) if first else (2, 8)))
     def _(o):
         rows = pl.ds(pl.multiple_of(o * 8, 8), 8)
         points = [(branch[0, b, rows, :], branch[1, b, rows, :]) for b in range(SLOW)]
         for k, (re, im) in enumerate(fft(points)):
-            c = jnp.broadcast_to(turn_ref[i, 0, k : k + 1, :], (8, FAST))
-            s = jnp.broadcast_to(turn_ref[i, 1, k : k + 1, :], (8, FAST))
+            c = jnp.broadcast_to(turn_ref[i, k : k + 1, :], (8, FAST))
+            s = jnp.broadcast_to(turn_ref[i, SLOW + k : SLOW + k + 1, :], (8, FAST))
             inner[k, rows, 0:FAST] = re * c + im * s
             inner[k, rows, FAST : 2 * FAST] = im * c - re * s
 
+
+def fast_transform(i, last_ref, inner, flat):
     @pl.loop(0, 8)
     def _(g):
         points = inner[pl.ds(g * 4, 4), :, :].reshape(4 * 64, 2 * FAST).astype(jnp.bfloat16)
@@ -183,11 +228,21 @@
 
 
 def whole_kernel(
-    pieces,
+    delays,
+    voltages_hbm,
+    tap_hbm,
+    turn_hbm,
+    last_hbm,
+    out_ref,
+    voltages,
+    tap_all,
+    turn_all,
+    last_all,
     taps_ref,
     turn_ref,
     last_ref,
-    out_ref,
+    spread,
+    pieces,
     own,
     halo,
     chunks,
@@ -198,6 +253,7 @@
     flat,
     wide,
     packed,
+    load_sem,
     near_send,
     near_recv,
     halo_send,
@@ -211,6 +267,15 @@
     me = tm * 4 + ct
     y, block, column = tm % 4, tm // 4, tm // 8
 
+    loads = [
+        pltpu.make_async_copy(voltages_hbm, voltages, load_sem.at[0]),
+        pltpu.make_async_copy(tap_hbm, tap_all, load_sem.at[1]),
+        pltpu.make_async_copy(turn_hbm, turn_all, load_sem.at[2]),
+        pltpu.make_async_copy(last_hbm, last_all, load_sem.at[3]),
+    ]
+    for load in loads:
+        load.start()
+
     barrier = pltpu.get_barrier_semaphore()
 
     @pl.loop(1, OWNERS)
@@ -226,42 +291,60 @@
     def _():
         halo[...] = jnp.zeros_like(halo)
 
+    loads[0].wait()
+    split_inputs(voltages, spread, pieces)
     pl.semaphore_wait(barrier, OWNERS)
 
-    def near(i, offset):
+    def near(i, r, offset):
         other = (y + offset) % GROUP
         return pltpu.make_async_remote_copy(
-            src_ref=pieces.at[other, i],
-            dst_ref=own.at[y, i],
-            send_sem=near_send.at[i, offset],
-            recv_sem=near_recv.at[i, y],
+            src_ref=pieces.at[other, i, r],
+            dst_ref=own.at[y, i, r],
+            send_sem=near_send.at[i, r, offset],
+            recv_sem=near_recv.at[i, r, y],
             device_id={"tm": block * 4 + other},
             device_id_type=MESH,
         )
 
-    def near_arrival(i, source):
-        return pltpu.make_async_copy(pieces.at[0, i], own.at[source, i], near_recv.at[i, source])
-
-    def halo_copy(i):
+    def near_arrival(i, r, source):
+        return pltpu.make_async_copy(
+            pieces.at[0, i, r], own.at[source, i, r], near_recv.at[i, r, source]
+        )
+
+    def halo_copy(i, r):
         return pltpu.make_async_remote_copy(
-            src_ref=own.at[GROUP - 1, i],
-            dst_ref=halo.at[i],
-            send_sem=halo_send.at[i],
-            recv_sem=halo_recv.at[i],
+            src_ref=own.at[GROUP - 1, i, r],
+            dst_ref=halo.at[i, r],
+            send_sem=halo_send.at[i, r],
+            recv_sem=halo_recv.at[i, r],
             device_id={"tm": (tm + GROUP) % 32},
             device_id_type=MESH,
         )
 
+    def pass_on(i):
+        for r in range(2):
+            near_arrival(i, r, GROUP - 1).wait()
+
+            @pl.when(block < 7)
+            def _():
+                halo_copy(i, r).start()
+
     for i in range(2):
-        pltpu.make_async_copy(pieces.at[y, i], own.at[y, i], near_recv.at[i, y]).start()
-        for offset in (1, 3, 2):
-            near(i, offset).start()
+        for r in range(2):
+            pltpu.make_async_copy(
+                pieces.at[y, i, r], own.at[y, i, r], near_recv.at[i, r, y]
+            ).start()
+            for offset in (1, 3, 2):
+                near(i, r, offset).start()
+
+    for load in loads[1:]:
+        load.wait()
     for i in range(2):
-        near_arrival(i, GROUP - 1).wait()
-
-        @pl.when(block < 7)
-        def _():
-            halo_copy(i).start()
+        delayed_tables(
+            i, delays[2 * y + i], tap_all, turn_all, last_all, taps_ref, turn_ref, last_ref
+        )
+        if i == 0:
+            pass_on(0)
 
     def far(l, i):
         return pltpu.make_async_remote_copy(
@@ -275,14 +358,25 @@
 
     @pl.loop(0, 2)
     def _(i):
-        for source in range(GROUP - 1):
-            near_arrival(i, source).wait()
+        for r in range(2):
+            for source in range(GROUP - 1):
+                near_arrival(i, r, source).wait()
+
+        filter_frames(i, own, halo, taps_ref, xs, branch, False)
+        slow_transform(i, turn_ref, branch, inner, False)
+
+        @pl.when(i == 0)
+        def _():
+            pass_on(1)
 
         @pl.when(block > 0)
         def _():
-            halo_copy(i).wait_recv()
-
-        filter_and_transform(i, own, halo, taps_ref, turn_ref, last_ref, xs, branch, inner, flat)
+            for r in range(2):
+                halo_copy(i, r).wait_recv()
+
+        filter_frames(i, own, halo, taps_ref, xs, branch, True)
+        slow_transform(i, turn_ref, branch, inner, True)
+        fast_transform(i, last_ref, inner, flat)
 
         @pl.loop(0, OWNERS, step=4)
         def _(j0):
@@ -337,12 +431,13 @@
     correlate(stn, packed, out_ref)
 
     for i in range(2):
-        for offset in (1, 3, 2):
-            near(i, offset).wait_send()
-
-        @pl.when(block < 7)
-        def _():
-            halo_copy(i).wait_send()
+        for r in range(2):
+            for offset in (1, 3, 2):
+                near(i, r, offset).wait_send()
+
+            @pl.when(block < 7)
+            def _():
+                halo_copy(i, r).wait_send()
 
     for p in range(4):
         twin(p).wait_send()
@@ -351,34 +446,38 @@
 
 
 def on_device(voltages, delays):
-    where = lax.axis_index("tm") % GROUP
-    mine = lax.dynamic_slice(delays, (2 * where,), (2,))
-    taps = jnp.stack([rolled_filter(mine[i]) for i in range(2)])
-    turn = jnp.stack([turn_tables(mine[i]) for i in range(2)])
-    last = jnp.stack([last_table(mine[i]) for i in range(2)])
-    pieces = voltages.reshape(2, GROUP, 2, BLOCK, CHANNELS).transpose(1, 2, 0, 3, 4)
     dma = pltpu.SemaphoreType.DMA
     f32, bf16 = jnp.float32, jnp.bfloat16
     return pl.pallas_call(
         whole_kernel,
         out_shape=jax.ShapeDtypeStruct((2, SLOW, 32, 64), f32),
-        in_specs=[pl.BlockSpec(memory_space=pltpu.VMEM)] * 4,
+        in_specs=[pl.BlockSpec(memory_space=pltpu.SMEM)] + [pl.BlockSpec(memory_space=pl.ANY)] * 4,
         out_specs=pl.BlockSpec(memory_space=pltpu.VMEM),
         scratch_shapes=[
+            pltpu.VMEM((2, 8, BLOCK * CHANNELS), bf16),
+            pltpu.VMEM((SLOW, TAPS, FAST), f32),
+            pltpu.VMEM((SLOW, 2 * SLOW, FAST), f32),
+            pltpu.VMEM((2 * FAST, 2 * FAST), f32),
+            pltpu.VMEM((2, SLOW, 24, FAST), f32),
+            pltpu.VMEM((2, 2 * SLOW, FAST), f32),
+            pltpu.VMEM((2, 2 * FAST, 2 * FAST), bf16),
+            pltpu.VMEM((2, 8 * BLOCK, FAST), f32),
+            pltpu.VMEM((GROUP, 2, 2, BLOCK, CHANNELS), bf16),
             pltpu.VMEM((GROUP, 2, 2, BLOCK, CHANNELS), bf16),
             pltpu.VMEM((2, 2, BLOCK, CHANNELS), bf16),
             pltpu.VMEM((OWNERS, 2, 2, 16, FAST), bf16),
             pltpu.VMEM((2, OWNERS, 2, 2, 16, FAST), bf16),
-            pltpu.VMEM((2, 80, FAST), f32),
+            pltpu.VMEM((2, 64, FAST), f32),
             pltpu.VMEM((2, SLOW, 64, FAST), f32),
             pltpu.VMEM((SLOW, 64, 2 * FAST), f32),
             pltpu.VMEM((2, FAST * 16, FAST), f32),
             pltpu.VMEM((2, 2, 64 * 16, FAST), f32),
             pltpu.VMEM((SLOW, FAST, 4 * FAST), bf16),
-            dma((2, GROUP)),
-            dma((2, GROUP)),
-            dma((2,)),
-            dma((2,)),
+            dma((4,)),
+            dma((2, 2, GROUP)),
+            dma((2, 2, GROUP)),
+            dma((2, 2)),
+            dma((2, 2)),
             dma,
             dma((4,)),
             dma((4,)),
@@ -387,7 +486,7 @@
         compiler_params=pltpu.CompilerParams(
             collective_id=0, has_side_effects=True, vmem_limit_bytes=56 << 20
         ),
-    )(pieces, taps, turn, last)
+    )(delays, voltages, tap_blocks(), turn_blocks(), last_table())
 
 
 def solution(mesh):

time: 124 us -> 103 us (0.83)
  other arithmetic: 5.87 us -> 0 us
  local copies, waits for them, and re-layouts: 7.47 us -> 2.26 us
  Pallas kernels: 106 us -> 101 us
  between operations: 4.17 us -> 0.01 us
    pallas_call x1, Pallas kernels: 106 us -> 101 us  [on_device(): pl.pallas_call(whole_kernel, out_shape=jax.ShapeDtypeStruct((2, SLOW, 32,...]
    another operation x6 -> x0, other arithmetic: 2.85 us -> none  [the longest x1 0.93 us: on_device(): taps = jnp.stack([rolled_filter(mine[i]) for i in range(2)])]
    unnamed x6 -> x1, local copies, waits for them, and re-layouts: 5.02 us -> 2.26 us
    reshape x3 -> x0, local copies, waits for them, and re-layouts: 1.52 us -> none  [the longest x1 1.47 us: on_device(): voltages.reshape(2, GROUP, 2, BLOCK, CHANNELS).transpose(1, 2, 0, 3, 4)]
    ge x2 -> x0, other arithmetic: 1.36 us -> none  [rolled_filter(): carry = jnp.arange(CHANNELS, dtype=jnp.int32) + delay >= CHANNELS]
    add x2 -> x0, other arithmetic: 1.35 us -> none  [turn_tables(): q + delay]
where the time goes in v3:
time: 103 us
  Pallas kernels  101 us (98%)
  local copies, waits for them, and re-layouts  2.26 us (2%)
    pallas_call x1, Pallas kernels, on_device(): pl.pallas_call(whole_kernel, out_shape=jax.ShapeDtypeStruct((2, SLOW, 32,...  101 us
    unnamed x1, local copies, waits for them, and re-layouts  2.26 us

profile of v3, /device:TPU:1, one launch (start us, length us, event | category | flops | bytes accessed | tf_op | source)
XLA Modules:
  0.0 103.1 jit_solution(15621347901192513755)
XLA Ops:
  0.0 100.8 %shard_map.55 = f32[2,32,32,64]{3,2,1,0:T(8,128)} custom-call(s32[8]{0:T(128)} %delays.1, bf16[2,8,65536]{2,1,0:T(8,128)(2,1)} %voltages_hbm.1, f32[32,16,128]{2,1,0:T(8,128)} %constant.6.clone.tap_hbm, f32[32,64,128]{2,1,0:T(8,128)} %constant.7.clone.turn_hbm, f32[256,256]{1,0:T(8,128)} %constant.8.clone.last_hbm), custom_call_target="tpu_custom_call" | custom-call | tf_op jit(solution)/shard_map/pallas_call | solution.py:451
  100.8 2.3 %copy.7 = f32[2,32,32,64]{3,2,1,0:T(8,128)} copy(f32[2,32,32,64]{3,2,1,0:T(8,128)} %shard_map.55) | data formatting | bytes 1048576

commit v4 on v3

--- a/solution.py
+++ b/solution.py
@@ -74,18 +74,17 @@
     return low + high
 
 
-def split_inputs(voltages, spread, pieces):
+def split_inputs(r, voltages, spread, pieces):
     @pl.loop(0, SLOW)
     def _(b):
         lanes = pl.ds(pl.multiple_of(b * FAST, FAST), FAST)
-        for r in range(2):
-            for f in range(BLOCK):
-                there = pl.ds(pl.multiple_of(f * CHANNELS + b * FAST, FAST), FAST)
-                spread[r, pl.ds(f, 8, stride=BLOCK), :] = voltages[r, :, there].astype(jnp.float32)
-        for r in range(2):
-            for i in range(8):
-                rows = spread[r, BLOCK * i : BLOCK * i + BLOCK, :]
-                pieces[i // 2, i % 2, r, :, lanes] = rows.astype(jnp.bfloat16)
+        slot = b % 2
+        for f in range(BLOCK):
+            there = pl.ds(pl.multiple_of(f * CHANNELS + b * FAST, FAST), FAST)
+            spread[slot, pl.ds(f, 8, stride=BLOCK), :] = voltages[r, :, there].astype(jnp.float32)
+        for i in range(8):
+            rows = spread[slot, BLOCK * i : BLOCK * i + BLOCK, :]
+            pieces[i // 2, i % 2, r, :, lanes] = rows.astype(jnp.bfloat16)
 
 
 def delayed_tables(i, delay, tap_ref, turn_all, last_all, taps_ref, turn_ref, last_ref):
@@ -173,9 +172,7 @@
                     flat[r, pl.ds(l * 128 + g * 2 + t, 8, stride=16), :] = piece
 
 
-def gather_pair(pair, got, wide, packed):
-    low = lax.broadcasted_iota(jnp.int32, (8, FAST), 1) < 64
-
+def widen(pair, got, wide):
     @pl.loop(0, 4)
     def _(step):
         t = step // 2
@@ -189,40 +186,49 @@
                         place = pl.ds(pl.multiple_of(row * 16, 16), 16)
                         wide[t, r, place, :] = got[stn, source, i, r, :, :].astype(jnp.float32)
 
-    lanes = pl.ds(pl.multiple_of(pair * FAST, FAST), FAST)
-
-    def reorder(j):
-        for r in range(2):
-            for g in range(4):
-                even, odd = [], []
-                for h in range(2):
-                    rows = pl.ds((g * 16 + h * 8) * 16 + j, 8, stride=16)
-                    a, b = wide[0, r, rows, :], wide[1, r, rows, :]
-                    crossed = pltpu.roll(jnp.where(low, b, a), 64, 1)
-                    even.append(jnp.where(low, a, crossed))
-                    odd.append(jnp.where(low, crossed, b))
-                place = slice(r * 64 + g * 16, r * 64 + g * 16 + 16)
-                packed[2 * j, place, lanes] = jnp.concatenate(even, axis=0).astype(jnp.bfloat16)
-                packed[2 * j + 1, place, lanes] = jnp.concatenate(odd, axis=0).astype(jnp.bfloat16)
+
+def reorder(j, lanes, wide, packed):
+    low = lax.broadcasted_iota(jnp.int32, (8, FAST), 1) < 64
+    for r in range(2):
+        for g in range(4):
+            even, odd = [], []
+            for h in range(2):
+                rows = pl.ds((g * 16 + h * 8) * 16 + j, 8, stride=16)
+                a, b = wide[0, r, rows, :], wide[1, r, rows, :]
+                crossed = pltpu.roll(jnp.where(low, b, a), 64, 1)
+                even.append(jnp.where(low, a, crossed))
+                odd.append(jnp.where(low, crossed, b))
+            place = slice(r * 64 + g * 16, r * 64 + g * 16 + 16)
+            packed[2 * j, place, lanes] = jnp.concatenate(even, axis=0).astype(jnp.bfloat16)
+            packed[2 * j + 1, place, lanes] = jnp.concatenate(odd, axis=0).astype(jnp.bfloat16)
+
+
+def products(k, mine, lanes, packed):
+    left = jnp.concatenate(
+        [packed[k, pl.ds(pl.multiple_of(r * 64 + mine * 32, 32), 32), lanes] for r in range(2)], axis=0
+    )
+    return lax.dot_general(
+        left, packed[k, :, lanes], (((1,), (1,)), ((), ())), preferred_element_type=jnp.float32
+    )
+
+
+def first_three(mine, packed, sums):
+    @pl.loop(0, SLOW, step=4)
+    def _(k0):
+        for u in range(4):
+            sums[k0 + u] = products(k0 + u, mine, slice(0, 3 * FAST), packed)
+
+
+def last_one(mine, wide, packed, sums, out_ref):
+    lanes = slice(3 * FAST, 4 * FAST)
 
     @pl.loop(0, 16, step=4)
     def _(j0):
         for u in range(4):
-            reorder(j0 + u)
-
-
-def correlate(mine, packed, out_ref):
-    @pl.loop(0, SLOW, step=4)
-    def _(k0):
-        for u in range(4):
-            k = k0 + u
-            left = jnp.concatenate(
-                [packed[k, pl.ds(pl.multiple_of(r * 64 + mine * 32, 32), 32), :] for r in range(2)],
-                axis=0,
-            )
-            grid = lax.dot_general(
-                left, packed[k], (((1,), (1,)), ((), ())), preferred_element_type=jnp.float32
-            )
+            reorder(j0 + u, lanes, wide, packed)
+        for u in range(8):
+            k = 2 * j0 + u
+            grid = sums[k] + products(k, mine, lanes, packed)
             out_ref[0, k, :, :] = (grid[0:32, 0:64] + grid[32:64, 64:128]) * (1.0 / FRAMES)
             out_ref[1, k, :, :] = (grid[32:64, 0:64] - grid[0:32, 64:128]) * (1.0 / FRAMES)
 
@@ -253,7 +259,9 @@
     flat,
     wide,
     packed,
+    sums,
     load_sem,
+    all_sem,
     near_send,
     near_recv,
     halo_send,
@@ -268,32 +276,39 @@
     y, block, column = tm % 4, tm // 4, tm // 8
 
     loads = [
-        pltpu.make_async_copy(voltages_hbm, voltages, load_sem.at[0]),
-        pltpu.make_async_copy(tap_hbm, tap_all, load_sem.at[1]),
-        pltpu.make_async_copy(turn_hbm, turn_all, load_sem.at[2]),
-        pltpu.make_async_copy(last_hbm, last_all, load_sem.at[3]),
+        pltpu.make_async_copy(voltages_hbm.at[0], voltages.at[0], load_sem.at[0]),
+        pltpu.make_async_copy(voltages_hbm.at[1], voltages.at[1], load_sem.at[1]),
+        pltpu.make_async_copy(tap_hbm, tap_all, load_sem.at[2]),
+        pltpu.make_async_copy(turn_hbm, turn_all, load_sem.at[3]),
+        pltpu.make_async_copy(last_hbm, last_all, load_sem.at[4]),
     ]
     for load in loads:
         load.start()
 
+    def along_y(offset):
+        return {"tm": block * 4 + (y + offset) % 4, "ct": ct}
+
+    def along_z(offset):
+        z = ((block % 2) * 4 + ct + offset) % 8
+        return {"tm": column * 8 + (z // 4) * 4 + y, "ct": z % 4}
+
+    def along_x(offset):
+        return {"tm": (tm + 8 * offset) % 32, "ct": ct}
+
+    diagonal = {"tm": (tm + jnp.where(block % 2 == 0, 28, 4)) % 32, "ct": ct}
+    greeted = [along_y(o) for o in range(1, 4)] + [{"stn": 1 - stn}, diagonal]
+    greeted += [along_z(o) for o in range(1, 8)] + [along_x(o) for o in range(1, 4)]
     barrier = pltpu.get_barrier_semaphore()
-
-    @pl.loop(1, OWNERS)
-    def _(j):
-        l = (me + j) % OWNERS
-        pl.semaphore_signal(
-            barrier, inc=1, device_id={"tm": l // 4, "ct": l % 4}, device_id_type=MESH
-        )
-
-    pl.semaphore_signal(barrier, inc=1, device_id={"stn": 1 - stn}, device_id_type=MESH)
+    for other in greeted:
+        pl.semaphore_signal(barrier, inc=1, device_id=other, device_id_type=MESH)
 
     @pl.when(block == 0)
     def _():
         halo[...] = jnp.zeros_like(halo)
 
     loads[0].wait()
-    split_inputs(voltages, spread, pieces)
-    pl.semaphore_wait(barrier, OWNERS)
+    split_inputs(0, voltages, spread, pieces)
+    pl.semaphore_wait(barrier, len(greeted))
 
     def near(i, r, offset):
         other = (y + offset) % GROUP
@@ -329,15 +344,25 @@
             def _():
                 halo_copy(i, r).start()
 
-    for i in range(2):
-        for r in range(2):
-            pltpu.make_async_copy(
-                pieces.at[y, i, r], own.at[y, i, r], near_recv.at[i, r, y]
-            ).start()
-            for offset in (1, 3, 2):
-                near(i, r, offset).start()
-
-    for load in loads[1:]:
+    def exchange(i, r):
+        pltpu.make_async_copy(pieces.at[y, i, r], own.at[y, i, r], near_recv.at[i, r, y]).start()
+        for offset in (1, 3, 2):
+            near(i, r, offset).start()
+
+    exchange(0, 0)
+    loads[1].wait()
+    split_inputs(1, voltages, spread, pieces)
+    exchange(0, 1)
+    exchange(1, 0)
+    exchange(1, 1)
+
+    for offset in range(1, 8):
+        pl.semaphore_signal(all_sem.at[0], inc=1, device_id=along_z(offset), device_id_type=MESH)
+    pl.semaphore_wait(all_sem.at[0], 7)
+    for offset in range(1, 4):
+        pl.semaphore_signal(all_sem.at[1], inc=1, device_id=along_y(offset), device_id_type=MESH)
+
+    for load in loads[2:]:
         load.wait()
     for i in range(2):
         delayed_tables(
@@ -377,6 +402,10 @@
         filter_frames(i, own, halo, taps_ref, xs, branch, True)
         slow_transform(i, turn_ref, branch, inner, True)
         fast_transform(i, last_ref, inner, flat)
+
+        @pl.when(i == 0)
+        def _():
+            pl.semaphore_wait(all_sem.at[1], 3)
 
         @pl.loop(0, OWNERS, step=4)
         def _(j0):
@@ -417,18 +446,22 @@
 
     hand_over((column + 3) % 4)
 
-    @pl.loop(0, 4)
-    def _(step):
+    for step in range(4):
         p = (column + 3 - step) % 4
-
-        @pl.when(step < 3)
-        def _():
-            hand_over((column + 2 - step + 4) % 4)
-
+        if step < 3:
+            hand_over((column + 2 - step) % 4)
         twin(p).wait_recv()
-        gather_pair(p, got, wide, packed)
-
-    correlate(stn, packed, out_ref)
+        widen(p, got, wide)
+        if step < 3:
+
+            @pl.loop(0, 16, step=4)
+            def _(j0):
+                for u in range(4):
+                    reorder(j0 + u, slice(step * FAST, step * FAST + FAST), wide, packed)
+
+        if step == 2:
+            first_three(stn, packed, sums)
+    last_one(stn, wide, packed, sums, out_ref)
 
     for i in range(2):
         for r in range(2):
@@ -473,7 +506,9 @@
             pltpu.VMEM((2, FAST * 16, FAST), f32),
             pltpu.VMEM((2, 2, 64 * 16, FAST), f32),
             pltpu.VMEM((SLOW, FAST, 4 * FAST), bf16),
-            dma((4,)),
+            pltpu.VMEM((SLOW, 64, FAST), f32),
+            dma((5,)),
+            pltpu.SemaphoreType.REGULAR((2,)),
             dma((2, 2, GROUP)),
             dma((2, 2, GROUP)),
             dma((2, 2)),

time: 103 us -> 101 us (0.981)
  Pallas kernels: 101 us -> 98 us
    pallas_call x1, Pallas kernels: 101 us -> 98 us  [on_device(): pl.pallas_call(whole_kernel, out_shape=jax.ShapeDtypeStruct((2, SLOW, 32,...]
where the time goes in v4:
time: 101 us; the launch traced here: 100 us
  Pallas kernels  98 us (97%)
  local copies, waits for them, and re-layouts  2.26 us (2%)
    pallas_call x1, Pallas kernels, on_device(): pl.pallas_call(whole_kernel, out_shape=jax.ShapeDtypeStruct((2, SLOW, 32,...  98 us
    unnamed x1, local copies, waits for them, and re-layouts  2.26 us

profile of v4, /device:TPU:1, one launch (start us, length us, event | category | flops | bytes accessed | tf_op | source)
XLA Modules:
  0.0 100.2 jit_solution(10864379030447517195)
XLA Ops:
  0.0 98.0 %shard_map.55 = f32[2,32,32,64]{3,2,1,0:T(8,128)} custom-call(s32[8]{0:T(128)} %delays.1, bf16[2,8,65536]{2,1,0:T(8,128)(2,1)} %voltages_hbm.1, f32[32,16,128]{2,1,0:T(8,128)} %constant.6.clone.tap_hbm, f32[32,64,128]{2,1,0:T(8,128)} %constant.7.clone.turn_hbm, f32[256,256]{1,0:T(8,128)} %constant.8.clone.last_hbm), custom_call_target="tpu_custom_call" | custom-call | tf_op jit(solution)/shard_map/pallas_call | solution.py:484
  98.0 2.3 %copy.7 = f32[2,32,32,64]{3,2,1,0:T(8,128)} copy(f32[2,32,32,64]{3,2,1,0:T(8,128)} %shard_map.55) | data formatting | bytes 1048576

commit v5 on v4

--- a/solution.py
+++ b/solution.py
@@ -172,65 +172,71 @@
                     flat[r, pl.ds(l * 128 + g * 2 + t, 8, stride=16), :] = piece
 
 
-def widen(pair, got, wide):
-    @pl.loop(0, 4)
-    def _(step):
-        t = step // 2
-        stn = step % 2
+def widen(block, got, wide):
+    @pl.loop(0, 2)
+    def _(stn):
         for ct in range(4):
             for y in range(4):
                 for i in range(2):
                     for r in range(2):
                         row = stn * 32 + (ct * 4 + y) * 2 + i
-                        source = (pair * 2 + t) * 16 + y * 4 + ct
                         place = pl.ds(pl.multiple_of(row * 16, 16), 16)
-                        wide[t, r, place, :] = got[stn, source, i, r, :, :].astype(jnp.float32)
+                        wide[r, place, :] = got[stn, block * 16 + y * 4 + ct, i, r, :, :].astype(
+                            jnp.float32
+                        )
 
 
 def reorder(j, lanes, wide, packed):
-    low = lax.broadcasted_iota(jnp.int32, (8, FAST), 1) < 64
     for r in range(2):
         for g in range(4):
-            even, odd = [], []
-            for h in range(2):
-                rows = pl.ds((g * 16 + h * 8) * 16 + j, 8, stride=16)
-                a, b = wide[0, r, rows, :], wide[1, r, rows, :]
-                crossed = pltpu.roll(jnp.where(low, b, a), 64, 1)
-                even.append(jnp.where(low, a, crossed))
-                odd.append(jnp.where(low, crossed, b))
+            rows = [wide[r, pl.ds((g * 16 + h * 8) * 16 + j, 8, stride=16), :] for h in range(2)]
             place = slice(r * 64 + g * 16, r * 64 + g * 16 + 16)
-            packed[2 * j, place, lanes] = jnp.concatenate(even, axis=0).astype(jnp.bfloat16)
-            packed[2 * j + 1, place, lanes] = jnp.concatenate(odd, axis=0).astype(jnp.bfloat16)
-
-
-def products(k, mine, lanes, packed):
-    left = jnp.concatenate(
-        [packed[k, pl.ds(pl.multiple_of(r * 64 + mine * 32, 32), 32), lanes] for r in range(2)], axis=0
-    )
-    return lax.dot_general(
-        left, packed[k, :, lanes], (((1,), (1,)), ((), ())), preferred_element_type=jnp.float32
-    )
-
-
-def first_three(mine, packed, sums):
-    @pl.loop(0, SLOW, step=4)
-    def _(k0):
-        for u in range(4):
-            sums[k0 + u] = products(k0 + u, mine, slice(0, 3 * FAST), packed)
-
-
-def last_one(mine, wide, packed, sums, out_ref):
-    lanes = slice(3 * FAST, 4 * FAST)
+            packed[j, place, lanes] = jnp.concatenate(rows, axis=0).astype(jnp.bfloat16)
+
+
+def reorder_all(step, wide, packed):
+    lanes = pl.ds(pl.multiple_of(step * FAST, FAST), FAST)
 
     @pl.loop(0, 16, step=4)
     def _(j0):
         for u in range(4):
             reorder(j0 + u, lanes, wide, packed)
-        for u in range(8):
-            k = 2 * j0 + u
-            grid = sums[k] + products(k, mine, lanes, packed)
-            out_ref[0, k, :, :] = (grid[0:32, 0:64] + grid[32:64, 64:128]) * (1.0 / FRAMES)
-            out_ref[1, k, :, :] = (grid[32:64, 0:64] - grid[0:32, 64:128]) * (1.0 / FRAMES)
+
+
+def products(j, mine, begin, end, packed):
+    lanes = slice(begin * FAST, end * FAST)
+    shape = (64, (end - begin) * FAST)
+    even = (lax.broadcasted_iota(jnp.int32, shape, 1) % FAST < 64).astype(jnp.float32)
+    even = even.astype(jnp.bfloat16)
+    left = jnp.concatenate(
+        [packed[j, pl.ds(pl.multiple_of(r * 64 + mine * 32, 32), 32), lanes] for r in range(2)], axis=0
+    )
+    left = jnp.concatenate([left * even, left * (1 - even)], axis=0)
+    return lax.dot_general(
+        left, packed[j, :, lanes], (((1,), (1,)), ((), ())), preferred_element_type=jnp.float32
+    )
+
+
+def first_six(mine, packed, sums):
+    @pl.loop(0, 16, step=2)
+    def _(j0):
+        for u in range(2):
+            sums[j0 + u] = products(j0 + u, mine, 0, 6, packed)
+
+
+def last_two(mine, wide, packed, sums, out_ref):
+    @pl.loop(0, 16, step=4)
+    def _(j0):
+        for u in range(4):
+            reorder(j0 + u, slice(7 * FAST, 8 * FAST), wide, packed)
+        for u in range(4):
+            j = j0 + u
+            both = sums[j] + products(j, mine, 6, 8, packed)
+            for odd in range(2):
+                grid = both[64 * odd : 64 * odd + 64]
+                k = 2 * j + odd
+                out_ref[0, k, :, :] = (grid[0:32, 0:64] + grid[32:64, 64:128]) * (1.0 / FRAMES)
+                out_ref[1, k, :, :] = (grid[32:64, 0:64] - grid[0:32, 64:128]) * (1.0 / FRAMES)
 
 
 def whole_kernel(
@@ -353,8 +359,6 @@
     loads[1].wait()
     split_inputs(1, voltages, spread, pieces)
     exchange(0, 1)
-    exchange(1, 0)
-    exchange(1, 1)
 
     for offset in range(1, 8):
         pl.semaphore_signal(all_sem.at[0], inc=1, device_id=along_z(offset), device_id_type=MESH)
@@ -376,7 +380,7 @@
             src_ref=chunks.at[l, i],
             dst_ref=got.at[stn, me, i],
             send_sem=far_send,
-            recv_sem=far_recv.at[column],
+            recv_sem=far_recv.at[block],
             device_id={"tm": l // 4, "ct": l % 4},
             device_id_type=MESH,
         )
@@ -386,6 +390,10 @@
         for r in range(2):
             for source in range(GROUP - 1):
                 near_arrival(i, r, source).wait()
+
+            @pl.when(i == 0)
+            def _():
+                exchange(1, r)
 
         filter_frames(i, own, halo, taps_ref, xs, branch, False)
         slow_transform(i, turn_ref, branch, inner, False)
@@ -418,7 +426,7 @@
             @pl.when(j0 == 0)
             def _():
                 pltpu.make_async_copy(
-                    chunks.at[me, i], got.at[stn, me, i], far_recv.at[column]
+                    chunks.at[me, i], got.at[stn, me, i], far_recv.at[block]
                 ).start()
 
             @pl.when(j0 > 0)
@@ -429,7 +437,7 @@
                 far((me + j0 + u) % OWNERS, i).start()
 
     def twin(p):
-        rows = got.at[stn, pl.ds(p * 32, 32)]
+        rows = got.at[stn, pl.ds(p * 16, 16)]
         return pltpu.make_async_remote_copy(
             src_ref=rows,
             dst_ref=rows,
@@ -439,29 +447,36 @@
             device_id_type=MESH,
         )
 
-    def hand_over(p):
-        rows = got.at[stn, pl.ds(p * 32, 32)]
-        pltpu.make_async_copy(rows, rows, far_recv.at[p]).wait()
-        twin(p).start()
-
-    hand_over((column + 3) % 4)
-
-    for step in range(4):
-        p = (column + 3 - step) % 4
-        if step < 3:
-            hand_over((column + 2 - step) % 4)
-        twin(p).wait_recv()
-        widen(p, got, wide)
-        if step < 3:
-
-            @pl.loop(0, 16, step=4)
-            def _(j0):
-                for u in range(4):
-                    reorder(j0 + u, slice(step * FAST, step * FAST + FAST), wide, packed)
-
-        if step == 2:
-            first_three(stn, packed, sums)
-    last_one(stn, wide, packed, sums, out_ref)
+    def turn(step):
+        return (block + 7 - step) % 8
+
+    def hand_over(step):
+        rows = got.at[stn, pl.ds(turn(step) * 16, 16)]
+        pltpu.make_async_copy(rows, rows, far_recv.at[turn(step)]).wait()
+        twin(turn(step)).start()
+
+    def take(step):
+        twin(turn(step)).wait_recv()
+        widen(turn(step), got, wide)
+
+    hand_over(0)
+
+    @pl.loop(0, 6)
+    def _(step):
+        @pl.when(step < 5)
+        def _():
+            hand_over(step + 1)
+
+        take(step)
+        reorder_all(step, wide, packed)
+
+    first_six(stn, packed, sums)
+    hand_over(6)
+    hand_over(7)
+    take(6)
+    reorder_all(6, wide, packed)
+    take(7)
+    last_two(stn, wide, packed, sums, out_ref)
 
     for i in range(2):
         for r in range(2):
@@ -472,7 +487,7 @@
             def _():
                 halo_copy(i, r).wait_send()
 
-    for p in range(4):
+    for p in range(8):
         twin(p).wait_send()
     sent = chunks.at[pl.ds(0, OWNERS - 1)]
     pltpu.make_async_copy(sent, sent, far_send).wait()
@@ -504,9 +519,9 @@
             pltpu.VMEM((2, SLOW, 64, FAST), f32),
             pltpu.VMEM((SLOW, 64, 2 * FAST), f32),
             pltpu.VMEM((2, FAST * 16, FAST), f32),
-            pltpu.VMEM((2, 2, 64 * 16, FAST), f32),
-            pltpu.VMEM((SLOW, FAST, 4 * FAST), bf16),
-            pltpu.VMEM((SLOW, 64, FAST), f32),
+            pltpu.VMEM((2, 64 * 16, FAST), f32),
+            pltpu.VMEM((16, FAST, 8 * FAST), bf16),
+            pltpu.VMEM((16, FAST, FAST), f32),
             dma((5,)),
             pltpu.SemaphoreType.REGULAR((2,)),
             dma((2, 2, GROUP)),
@@ -514,9 +529,9 @@
             dma((2, 2)),
             dma((2, 2)),
             dma,
-            dma((4,)),
-            dma((4,)),
-            dma((4,)),
+            dma((8,)),
+            dma((8,)),
+            dma((8,)),
         ],
         compiler_params=pltpu.CompilerParams(
             collective_id=0, has_side_effects=True, vmem_limit_bytes=56 << 20

time: 101 us -> 99.4 us (0.984)
  Pallas kernels: 98 us -> 95.8 us
    pallas_call x1, Pallas kernels: 98 us -> 95.8 us  [on_device(): pl.pallas_call(whole_kernel, out_shape=jax.ShapeDtypeStruct((2, SLOW, 32,...]
where the time goes in v5:
time: 99.4 us; the launch traced here: 98.1 us
  Pallas kernels  95.8 us (96%)
  local copies, waits for them, and re-layouts  2.26 us (2%)
    pallas_call x1, Pallas kernels, on_device(): pl.pallas_call(whole_kernel, out_shape=jax.ShapeDtypeStruct((2, SLOW, 32,...  95.8 us
    unnamed x1, local copies, waits for them, and re-layouts  2.26 us

profile of v5, /device:TPU:1, one launch (start us, length us, event | category | flops | bytes accessed | tf_op | source)
XLA Modules:
  0.0 98.1 jit_solution(9860553532723757549)
XLA Ops:
  0.0 95.8 %shard_map.55 = f32[2,32,32,64]{3,2,1,0:T(8,128)} custom-call(s32[8]{0:T(128)} %delays.1, bf16[2,8,65536]{2,1,0:T(8,128)(2,1)} %voltages_hbm.1, f32[32,16,128]{2,1,0:T(8,128)} %constant.6.clone.tap_hbm, f32[32,64,128]{2,1,0:T(8,128)} %constant.7.clone.turn_hbm, f32[256,256]{1,0:T(8,128)} %constant.8.clone.last_hbm), custom_call_target="tpu_custom_call" | custom-call | tf_op jit(solution)/shard_map/pallas_call | solution.py:499
  95.9 2.3 %copy.7 = f32[2,32,32,64]{3,2,1,0:T(8,128)} copy(f32[2,32,32,64]{3,2,1,0:T(8,128)} %shard_map.55) | data formatting | bytes 1048576

commit v6 on v5

--- a/solution.py
+++ b/solution.py
@@ -360,6 +360,12 @@
     split_inputs(1, voltages, spread, pieces)
     exchange(0, 1)
 
+    @pl.when(y == GROUP - 1)
+    def _():
+        exchange(1, 0)
+        exchange(1, 1)
+
+
     for offset in range(1, 8):
         pl.semaphore_signal(all_sem.at[0], inc=1, device_id=along_z(offset), device_id_type=MESH)
     pl.semaphore_wait(all_sem.at[0], 7)
@@ -391,7 +397,7 @@
             for source in range(GROUP - 1):
                 near_arrival(i, r, source).wait()
 
-            @pl.when(i == 0)
+            @pl.when((i == 0) & (y < GROUP - 1))
             def _():
                 exchange(1, r)
 

time: 99.4 us -> 99.2 us (level)
  no operation moved by 1% of the time
where the time goes in v6:
time: 99.2 us; the launch traced here: 97.9 us
  Pallas kernels  95.7 us (96%)
  local copies, waits for them, and re-layouts  2.26 us (2%)
    pallas_call x1, Pallas kernels, on_device(): pl.pallas_call(whole_kernel, out_shape=jax.ShapeDtypeStruct((2, SLOW, 32,...  95.7 us
    unnamed x1, local copies, waits for them, and re-layouts  2.26 us

profile of v6, /device:TPU:1, one launch (start us, length us, event | category | flops | bytes accessed | tf_op | source)
XLA Modules:
  0.0 97.9 jit_solution(3453476434190641058)
XLA Ops:
  0.0 95.7 %shard_map.55 = f32[2,32,32,64]{3,2,1,0:T(8,128)} custom-call(s32[8]{0:T(128)} %delays.1, bf16[2,8,65536]{2,1,0:T(8,128)(2,1)} %voltages_hbm.1, f32[32,16,128]{2,1,0:T(8,128)} %constant.6.clone.tap_hbm, f32[32,64,128]{2,1,0:T(8,128)} %constant.7.clone.turn_hbm, f32[256,256]{1,0:T(8,128)} %constant.8.clone.last_hbm), custom_call_target="tpu_custom_call" | custom-call | tf_op jit(solution)/shard_map/pallas_call | solution.py:505
  95.7 2.3 %copy.7 = f32[2,32,32,64]{3,2,1,0:T(8,128)} copy(f32[2,32,32,64]{3,2,1,0:T(8,128)} %shard_map.55) | data formatting | bytes 1048576

commit v7 on v6

--- a/solution.py
+++ b/solution.py
@@ -515,7 +515,7 @@
             pltpu.VMEM((2, SLOW, 24, FAST), f32),
             pltpu.VMEM((2, 2 * SLOW, FAST), f32),
             pltpu.VMEM((2, 2 * FAST, 2 * FAST), bf16),
-            pltpu.VMEM((2, 8 * BLOCK, FAST), f32),
+            pltpu.VMEM((2, 8 * BLOCK + BLOCK, FAST), f32),
             pltpu.VMEM((GROUP, 2, 2, BLOCK, CHANNELS), bf16),
             pltpu.VMEM((GROUP, 2, 2, BLOCK, CHANNELS), bf16),
             pltpu.VMEM((2, 2, BLOCK, CHANNELS), bf16),
@@ -524,8 +524,8 @@
             pltpu.VMEM((2, 64, FAST), f32),
             pltpu.VMEM((2, SLOW, 64, FAST), f32),
             pltpu.VMEM((SLOW, 64, 2 * FAST), f32),
-            pltpu.VMEM((2, FAST * 16, FAST), f32),
-            pltpu.VMEM((2, 64 * 16, FAST), f32),
+            pltpu.VMEM((2, FAST * 16 + 16, FAST), f32),
+            pltpu.VMEM((2, 64 * 16 + 16, FAST), f32),
             pltpu.VMEM((16, FAST, 8 * FAST), bf16),
             pltpu.VMEM((16, FAST, FAST), f32),
             dma((5,)),

time: 99.2 us -> 99.2 us (level)
  no operation moved by 1% of the time
where the time goes in v7:
time: 99.2 us; the launch traced here: 98 us
  Pallas kernels  95.7 us (96%)
  local copies, waits for them, and re-layouts  2.26 us (2%)
    pallas_call x1, Pallas kernels, on_device(): pl.pallas_call(whole_kernel, out_shape=jax.ShapeDtypeStruct((2, SLOW, 32,...  95.7 us
    unnamed x1, local copies, waits for them, and re-layouts  2.26 us

profile of v7, /device:TPU:1, one launch (start us, length us, event | category | flops | bytes accessed | tf_op | source)
XLA Modules:
  0.0 98.0 jit_solution(8853005073930601825)
XLA Ops:
  0.0 95.7 %shard_map.55 = f32[2,32,32,64]{3,2,1,0:T(8,128)} custom-call(s32[8]{0:T(128)} %delays.1, bf16[2,8,65536]{2,1,0:T(8,128)(2,1)} %voltages_hbm.1, f32[32,16,128]{2,1,0:T(8,128)} %constant.6.clone.tap_hbm, f32[32,64,128]{2,1,0:T(8,128)} %constant.7.clone.turn_hbm, f32[256,256]{1,0:T(8,128)} %constant.8.clone.last_hbm), custom_call_target="tpu_custom_call" | custom-call | tf_op jit(solution)/shard_map/pallas_call | solution.py:505
  95.7 2.3 %copy.7 = f32[2,32,32,64]{3,2,1,0:T(8,128)} copy(f32[2,32,32,64]{3,2,1,0:T(8,128)} %shard_map.55) | data formatting | bytes 1048576

commit v8 on v7

--- a/solution.py
+++ b/solution.py
@@ -225,11 +225,11 @@
 
 
 def last_two(mine, wide, packed, sums, out_ref):
-    @pl.loop(0, 16, step=4)
+    @pl.loop(0, 16, step=8)
     def _(j0):
-        for u in range(4):
+        for u in range(8):
             reorder(j0 + u, slice(7 * FAST, 8 * FAST), wide, packed)
-        for u in range(4):
+        for u in range(8):
             j = j0 + u
             both = sums[j] + products(j, mine, 6, 8, packed)
             for odd in range(2):

time: 99.2 us -> 98.7 us (level)
  no operation moved by 1% of the time
where the time goes in v8:
time: 98.7 us; the launch traced here: 97.5 us
  Pallas kernels  95.2 us (96%)
  local copies, waits for them, and re-layouts  2.26 us (2%)
    pallas_call x1, Pallas kernels, on_device(): pl.pallas_call(whole_kernel, out_shape=jax.ShapeDtypeStruct((2, SLOW, 32,...  95.2 us
    unnamed x1, local copies, waits for them, and re-layouts  2.26 us

profile of v8, /device:TPU:1, one launch (start us, length us, event | category | flops | bytes accessed | tf_op | source)
XLA Modules:
  0.0 97.5 jit_solution(1133041060212440758)
XLA Ops:
  0.0 95.2 %shard_map.55 = f32[2,32,32,64]{3,2,1,0:T(8,128)} custom-call(s32[8]{0:T(128)} %delays.1, bf16[2,8,65536]{2,1,0:T(8,128)(2,1)} %voltages_hbm.1, f32[32,16,128]{2,1,0:T(8,128)} %constant.6.clone.tap_hbm, f32[32,64,128]{2,1,0:T(8,128)} %constant.7.clone.turn_hbm, f32[256,256]{1,0:T(8,128)} %constant.8.clone.last_hbm), custom_call_target="tpu_custom_call" | custom-call | tf_op jit(solution)/shard_map/pallas_call | solution.py:505
  95.2 2.3 %copy.7 = f32[2,32,32,64]{3,2,1,0:T(8,128)} copy(f32[2,32,32,64]{3,2,1,0:T(8,128)} %shard_map.55) | data formatting | bytes 1048576
